TPU v7x, 32 devices: a whole 2x2x4 slice. The times are simulated.
32 devices in a mesh: dp: 2 (over core), seq: 16 (over z, y, x).
Axes of the slice: x: 2, y: 2, z: 4, core: 2. Of those that a mesh axis runs over, the one named last changes fastest.
Arguments:
- loaded: bfloat16 [8192, 1024], P(('dp', 'seq')), may hold values from -6 to 6
- plan: int32 [32, 32], replicated, may hold values from 4 to 16, as said below
- segment_ids: int32 [4, 2048], P('dp'), may hold values from 0 to 31, never falling along the last dimension, each value on 1 to 1024 neighbouring positions
- in_weight: bfloat16 [1024, 2048], P('dp'), may hold values from -0.1875 to 0.1875
- out_weight: bfloat16 [1024, 1024], P('dp'), may hold values from -0.1875 to 0.1875
- depth_kernel: bfloat16 [1024, 31], P('dp'), may hold values from -2 to 2
- norm_gains: bfloat16 [1024, 2], P('dp'), may hold values from 0.25 to 1.75
- upstream: bfloat16 [4, 2048, 1024], P('dp', 'seq'), may hold values from -6 to 6
Outputs:
- encoded: bfloat16 [4, 2048, 1024], P('dp', 'seq')
- grad_frames: bfloat16 [4, 2048, 1024], P('dp', 'seq')
- grad_in_weight: float32 [1024, 2048], P('dp')
- grad_out_weight: float32 [1024, 1024], P('dp')
- grad_kernel: float32 [1024, 31], P('dp')
- grad_gains: float32 [1024, 2], P('dp')
Inputs may be any that keep to these rules, and one draw needn't show every extreme that they name: Every row and every column of plan sums to 256; every row reaches 16.
All inputs are finite; a program needn't handle non-finite values.
Results may differ from a plain program's by a relative error of at most 0.006.
Values may be sent and summed in bfloat16 or wider, within the bound.
A program may use at most 128 MiB of HBM per device.

v0:
```python
import math

import jax
import jax.numpy as jnp
from jax import lax
from jax.sharding import PartitionSpec as P


def padded(block, sides, width):
    for axis, dim in sides:
        count = lax.axis_size(axis)
        forward = [(i, i + 1) for i in range(count - 1)]
        backward = [(target, source) for source, target in forward]
        low = lax.ppermute(
            lax.slice_in_dim(block, block.shape[dim] - width, None, axis=dim), axis, forward
        )
        high = lax.ppermute(lax.slice_in_dim(block, 0, width, axis=dim), axis, backward)
        block = jnp.concatenate([low, block, high], axis=dim)
    return block


def norm_rows(values, gain):
    average = jnp.mean(values, axis=-1, keepdims=True)
    centered = values - average
    spread = jnp.mean(centered * centered, axis=-1, keepdims=True)
    return centered * lax.rsqrt(spread + 1e-05) * gain


def mid_section(values, gain):
    normed = norm_rows(values, gain)
    return normed * jax.nn.sigmoid(normed)


def per_device(
    loaded, plan, segment_ids, in_weight, out_weight, depth_kernel, norm_gains, upstream
):
    rows_dev, width = loaded.shape
    devices = plan.shape[0]
    capacity = 2 * rows_dev // devices
    slabs, slab_len = segment_ids.shape
    frames_dev = slab_len // lax.axis_size("seq")
    kernel_len = depth_kernel.shape[1]
    margin = kernel_len // 2
    sender = lax.axis_index(("dp", "seq"))
    send_plan = lax.dynamic_index_in_dim(plan, sender, 0, keepdims=False)
    send_start = jnp.cumsum(send_plan) - send_plan
    slot_index = jnp.arange(capacity, dtype=jnp.int32)
    source_rows = send_start[:, None] + slot_index[None, :]
    filled = slot_index[None, :] < send_plan[:, None]
    picked = jnp.take(loaded, jnp.clip(source_rows, 0, rows_dev - 1).reshape(-1), axis=0)
    outgoing = jnp.where(filled.reshape(-1, 1), picked, jnp.zeros_like(picked)).reshape(
        devices, capacity, width
    )
    arrived = lax.all_to_all(
        outgoing, ("dp", "seq"), split_axis=0, concat_axis=0, tiled=True
    ).reshape(devices * capacity, width)
    recv_plan = lax.dynamic_index_in_dim(plan, sender, 1, keepdims=False)
    recv_end = jnp.cumsum(recv_plan)
    frame_index = jnp.arange(rows_dev, dtype=jnp.int32)
    before = recv_end[None, :] <= frame_index[:, None]
    source_dev = jnp.sum(before.astype(jnp.int32), axis=1)
    start_of = jnp.sum(jnp.where(before, recv_plan[None, :], 0), axis=1)
    frames = jnp.take(arrived, source_dev * capacity + frame_index - start_of, axis=0)
    kernel_full, gains_full = (
        lax.all_gather(depth_kernel, "dp", axis=0, tiled=True),
        lax.all_gather(norm_gains, "dp", axis=0, tiled=True),
    )
    taps = kernel_full.astype(jnp.float32)
    gain_pre = gains_full[:, 0].astype(jnp.float32)
    gain_mid = gains_full[:, 1].astype(jnp.float32)
    frame_rows = frames.astype(jnp.float32)
    normed_full, pull_pre = jax.vjp(norm_rows, frame_rows, gain_pre)
    normed = normed_full.astype(jnp.bfloat16)
    whole_in, whole_out = (
        lax.all_gather(in_weight, "dp", axis=0, tiled=True),
        lax.all_gather(out_weight, "dp", axis=0, tiled=True),
    )
    hidden = jnp.dot(normed, whole_in, preferred_element_type=jnp.float32)
    gate_lin = hidden[:, :width]
    gate_sig = jax.nn.sigmoid(hidden[:, width:])
    gated = (gate_lin * gate_sig).astype(jnp.bfloat16).reshape(slabs, frames_dev, width)
    gated_pad = padded(gated, (("seq", 1),), margin)
    id_pad = jnp.pad(segment_ids, ((0, 0), (margin, margin)), constant_values=-1)
    window = lax.dynamic_slice_in_dim(
        id_pad, lax.axis_index("seq") * frames_dev, frames_dev + 2 * margin, 1
    )
    center = window[:, margin : margin + frames_dev]
    mixing = jnp.zeros((slabs, frames_dev, width), jnp.float32)
    for tap_index in range(kernel_len):
        same = (window[:, tap_index : tap_index + frames_dev] == center)[..., None]
        mixing = mixing + jnp.where(
            same,
            gated_pad[:, tap_index : tap_index + frames_dev].astype(jnp.float32)
            * taps[:, tap_index],
            0.0,
        )
    activated_full, pull_mid = jax.vjp(mid_section, mixing.reshape(rows_dev, width), gain_mid)
    activated = activated_full.astype(jnp.bfloat16)
    upstream_rows = upstream.reshape(rows_dev, width)
    projected = jnp.dot(activated, whole_out, preferred_element_type=jnp.float32)
    grad_act = jnp.dot(upstream_rows, whole_out.T, preferred_element_type=jnp.float32)
    encoded = (frame_rows + projected).astype(jnp.bfloat16).reshape(slabs, frames_dev, width)
    grad_out_w = jnp.dot(activated.T, upstream_rows, preferred_element_type=jnp.float32)
    grad_mixing, grad_gain_mid = pull_mid(grad_act)
    grad_cells = grad_mixing.reshape(slabs, frames_dev, width)
    grad_pad = padded(grad_cells, (("seq", 1),), margin)
    grad_gated = jnp.zeros((slabs, frames_dev, width), jnp.float32)
    tap_grads = []
    for tap_index in range(kernel_len):
        same = (window[:, tap_index : tap_index + frames_dev] == center)[..., None]
        tap_grads.append(
            jnp.sum(
                jnp.where(
                    same,
                    grad_cells
                    * gated_pad[:, tap_index : tap_index + frames_dev].astype(jnp.float32),
                    0.0,
                ),
                axis=(0, 1),
            )
        )
        mirror = 2 * margin - tap_index
        back_same = (window[:, mirror : mirror + frames_dev] == center)[..., None]
        grad_gated = grad_gated + jnp.where(
            back_same, grad_pad[:, mirror : mirror + frames_dev] * taps[:, tap_index], 0.0
        )
    grad_taps = jnp.stack(tap_grads, axis=1)
    grad_gated = grad_gated.reshape(rows_dev, width)
    grad_hidden = jnp.concatenate(
        [grad_gated * gate_sig, grad_gated * gate_lin * gate_sig * (1.0 - gate_sig)], axis=1
    ).astype(jnp.bfloat16)
    grad_in_w = jnp.dot(normed.T, grad_hidden, preferred_element_type=jnp.float32)
    grad_normed = jnp.dot(grad_hidden, whole_in.T, preferred_element_type=jnp.float32)
    grad_rows, grad_gain_pre = pull_pre(grad_normed)
    grad_frames = (
        (upstream_rows.astype(jnp.float32) + grad_rows)
        .astype(jnp.bfloat16)
        .reshape(slabs, frames_dev, width)
    )
    grad_gain = jnp.stack([grad_gain_pre, grad_gain_mid], axis=1)
    shares = (
        lax.psum_scatter(grad_in_w, "dp", scatter_dimension=0, tiled=True),
        lax.psum_scatter(grad_out_w, "dp", scatter_dimension=0, tiled=True),
        lax.psum_scatter(grad_taps, "dp", scatter_dimension=0, tiled=True),
        lax.psum_scatter(grad_gain, "dp", scatter_dimension=0, tiled=True),
    )
    totals = lax.psum((shares[0], shares[1], shares[2], shares[3]), "seq")
    scale = 1.0 / math.sqrt(lax.axis_size("dp") * lax.axis_size("seq") * rows_dev)
    return (
        encoded,
        grad_frames,
        totals[0] * scale,
        totals[1] * scale,
        totals[2] * scale,
        totals[3] * scale,
    )


def solution(mesh):
    placed = (
        P(("dp", "seq"), None),
        P(),
        P("dp", None),
        P("dp", None),
        P("dp", None),
        P("dp", None),
        P("dp", None),
        P("dp", "seq", None),
    )
    return jax.shard_map(
        per_device,
        mesh=mesh,
        in_specs=placed,
        out_specs=(
            P("dp", "seq", None),
            P("dp", "seq", None),
            P("dp", None),
            P("dp", None),
            P("dp", None),
            P("dp", None),
        ),
        check_vma=False,
    )
```

profile of v0, /device:TPU:19, one launch (start us, length us, event | category | flops | bytes accessed | tf_op | source)
XLA Modules:
  0.0 569.0 jit_solution(17175301567011237490)
XLA Ops:
  8.4 2.1 gather_fusion
  10.6 1.2 select_select_fusion
  11.8 6.2 %all-to-all-start = ((bf16[32,16,1024]{2,1,0:T(8,128)(2,1)}), bf16[32,16,1024]{2,1,0:T(8,128)(2,1)S(1)}, u32[]{:S(2)}, u32[]{:S(2)}) async-start(bf16[32,16,1024]{2,1,0:T(8,128)(2,1)} %select_select_fusion), calls=%async_computation | async-start | bytes 2097152 | tf_op jit(solution)/shard_map/all_to_all | solution.py:54
  19.2 1.9 all_gather.12
  21.0 1.9 all_gather.14
  25.0 18.0 %all-to-all-done = bf16[32,16,1024]{2,1,0:T(8,128)(2,1)S(1)} async-done(((bf16[32,16,1024]{2,1,0:T(8,128)(2,1)}), bf16[32,16,1024]{2,1,0:T(8,128)(2,1)S(1)}, u32[]{:S(2)}, u32[]{:S(2)}) %all-to-all-start) | async-done | bytes 1048608 | tf_op jit(solution)/shard_map/all_to_all | solution.py:54
  43.0 1.2 gather_fusion.1
  44.8 3.6 fusion.332
  48.7 1.0 copy-done.2
  50.2 3.0 collective-permute-start
  53.3 2.2 collective-permute-start.1
  56.3 20.1 %collective-permute-done = bf16[2,15,1024]{1,2,0:T(8,128)(2,1)S(1)} collective-permute-done((bf16[2,15,1024]{1,2,0:T(8,128)(2,1)S(1)}, bf16[2,15,1024]{1,2,0:T(8,128)(2,1)S(1)}, u32[]{:S(2)}, u32[]{:S(2)}) %collective-permute-start) | collective-permute-done | bytes 61472 | tf_op jit(solution)/shard_map/ppermute | solution.py:14
  76.7 15.5 %fusion.337 = (f32[2,128]{1,0:T(2,128)S(1)}, f32[2,128,1024]{1,2,0:T(8,128)S(1)}) fusion(f32[1024]{0:T(1024)S(1)} %bitcast.163, bf16[2,15,1024]{1,2,0:T(8,128)(2,1)S(1)} %collective-permute-done.1, bf16[2,128,1024]{1,2,0:T(8,128)(2,1)S(1)} %copy.146, pred[2,128]{1,0:T(4,128)(4,1)} %get-tuple-element.128, f32[1024]{0:T(1024)S(1)} %bitcast.161, ...), kind=kLoop, calls=%fused_computation.600 | loop fusion | flops 55836416 | bytes 1831424 | tf_op jit(solution)/shard_map/jvp()/reduce_sum | solution.py:23
  92.2 1.3 copy.151
  93.8 4.0 multiply_reduce_fusion
  97.8 1.4 fusion.335
  100.3 1.0 copy-done.7
  101.3 1.6 copy.153
  103.1 4.8 collective-permute-start.3
  107.9 2.1 collective-permute-start.2
  110.0 4.6 fusion.86
  114.6 4.8 fusion.59
  119.5 4.8 fusion.77
  124.3 4.8 fusion.125
  129.5 4.7 fusion.128
  134.6 1.3 copy.157
  136.3 26.6 %fusion.137 = f32[2,128,1024]{1,2,0:T(8,128)} fusion(f32[2,15,1024]{1,2,0:T(8,128)} %copy.157, f32[2,128,1024]{1,2,0:T(8,128)S(1)} %copy.153, f32[2,15,1024]{1,2,0:T(8,128)S(1)} %copy.154, f32[1024]{0:T(1024)S(1)} %bitcast.164, f32[1024]{0:T(1024)S(1)} %bitcast.162, f32[1024]{0:T(1024)S(1)} %bitcast.160, f32[1024]{0:T(1024)S(1)} %bitcast.158, ...), kind=kLoop, calls=%fused_computation.319 | loop fusion | flops 31719424 | bytes 2477568 | tf_op jit(solution)/shard_map/add | solution.py:124
  162.9 2.7 copy.159
  165.6 1.9 fusion.254
  168.1 1.4 fusion.130
  170.6 1.0 copy.190
  172.0 2.6 stack.136
  174.8 3.9 convolution_bitcast_fusion
  178.7 1.0 copy-done.11
  179.7 4.8 fusion.259
  184.6 1.7 copy.191
  186.2 6.4 %reduce-scatter.11.cloned.1.call-done = f32[512,31]{0,1:T(8,128)} async-done(((f32[1024,31]{0,1:T(8,128)}), f32[512,31]{0,1:T(8,128)}) %reduce-scatter.11.cloned.1.call-update) | async-done | bytes 63504 | tf_op jit(solution)/shard_map/reduce_scatter | solution.py:144
  192.7 15.8 %reduce-scatter.9.cloned.1.call-done = f32[512,1024]{1,0:T(8,128)} async-done(((f32[1024,1024]{1,0:T(8,128)}), f32[512,1024]{1,0:T(8,128)}) %reduce-scatter.9.cloned.1.call-update) | async-done | bytes 2097168 | tf_op jit(solution)/shard_map/reduce_scatter | solution.py:143
  208.5 19.9 %reduce-scatter.7.cloned.1.call-done = f32[512,2048]{1,0:T(8,128)} async-done(((f32[1024,2048]{1,0:T(8,128)}), f32[512,2048]{1,0:T(8,128)}) %reduce-scatter.7.cloned.1.call-update) | async-done | bytes 4194320 | tf_op jit(solution)/shard_map/reduce_scatter | solution.py:142
  228.4 1.0 copy-done.12
  229.4 3.2 fusion.4
  232.6 1.3 add_convert_fusion
  233.8 102.6 %all-reduce.6.cloned.1.call-done = (f32[512,31]{0,1:T(8,128)}, f32[512,2]{0,1:T(2,128)}) async-done(((f32[512,31]{0,1:T(8,128)}, f32[512,2]{0,1:T(2,128)}), (f32[512,31]{0,1:T(8,128)}, f32[512,2]{0,1:T(2,128)})) %all-reduce.6.cloned.1.call-update) | async-done | bytes 67600 | tf_op jit(solution)/shard_map/psum | solution.py:147
  336.4 1.3 broadcast_multiply_fusion.3
  337.7 1.5 broadcast_multiply_fusion.2
  339.2 216.3 %all-reduce.8.cloned.1.call-done = (f32[512,2048]{1,0:T(8,128)}, f32[512,1024]{1,0:T(8,128)}) async-done(((f32[512,2048]{1,0:T(8,128)}, f32[512,1024]{1,0:T(8,128)}), (f32[512,2048]{1,0:T(8,128)}, f32[512,1024]{1,0:T(8,128)})) %all-reduce.8.cloned.1.call-update) | async-done | bytes 6291472 | tf_op jit(solution)/shard_map/psum | solution.py:147
  555.5 5.1 broadcast_multiply_fusion
  560.7 1.5 broadcast_multiply_fusion.1
  (358 shorter events, 10.1 us)
Async XLA Ops:
  7.2 37.6 %all-gather.3.cloned.1.call-start = ((), (), s32[]{:S(2)}) async-start(), calls=%async_computation.5 | async-start | bytes 6291456 | tf_op jit(solution)/shard_map/all_gather | solution.py:75
  11.8 31.2 %all-to-all-start = ((bf16[32,16,1024]{2,1,0:T(8,128)(2,1)}), bf16[32,16,1024]{2,1,0:T(8,128)(2,1)S(1)}, u32[]{:S(2)}, u32[]{:S(2)}) async-start(bf16[32,16,1024]{2,1,0:T(8,128)(2,1)} %select_select_fusion), calls=%async_computation | async-start | bytes 2097152 | tf_op jit(solution)/shard_map/all_to_all | solution.py:54
  18.0 75.8 %all-gather.5.cloned.1.call-start = ((), (), s32[]{:S(2)}) async-start(), calls=%async_computation.6 | async-start | bytes 3145728 | tf_op jit(solution)/shard_map/all_gather | solution.py:76
  18.7 165.8 %reduce-scatter.13.cloned.1.call-start = ((), (), s32[]{:S(2)}) async-start(), calls=%async_computation.10 | async-start | bytes 786432
  24.5 51.9 %copy-start.112 = (pred[2,128]{1,0:T(4,128)(4,1)}, pred[2,128]{1,0:T(4,128)(4,1)S(1)}, u32[]{:S(2)}) copy-start(pred[2,128]{1,0:T(4,128)(4,1)S(1)} %get-tuple-element.101) | copy-start | bytes 772
  24.5 51.9 %copy-start.115 = (pred[2,128]{1,0:T(4,128)(4,1)}, pred[2,128]{1,0:T(4,128)(4,1)S(1)}, u32[]{:S(2)}) copy-start(pred[2,128]{1,0:T(4,128)(4,1)S(1)} %get-tuple-element.102) | copy-start | bytes 772
  24.5 51.9 %copy-start.118 = (pred[2,128]{1,0:T(4,128)(4,1)}, pred[2,128]{1,0:T(4,128)(4,1)S(1)}, u32[]{:S(2)}) copy-start(pred[2,128]{1,0:T(4,128)(4,1)S(1)} %get-tuple-element.103) | copy-start | bytes 772
  24.5 51.9 %copy-start.121 = (pred[2,128]{1,0:T(4,128)(4,1)}, pred[2,128]{1,0:T(4,128)(4,1)S(1)}, u32[]{:S(2)}) copy-start(pred[2,128]{1,0:T(4,128)(4,1)S(1)} %get-tuple-element.104) | copy-start | bytes 772
  24.5 51.9 %copy-start.124 = (pred[2,128]{1,0:T(4,128)(4,1)}, pred[2,128]{1,0:T(4,128)(4,1)S(1)}, u32[]{:S(2)}) copy-start(pred[2,128]{1,0:T(4,128)(4,1)S(1)} %get-tuple-element.105) | copy-start | bytes 772
  24.6 51.9 %copy-start.127 = (pred[2,128]{1,0:T(4,128)(4,1)}, pred[2,128]{1,0:T(4,128)(4,1)S(1)}, u32[]{:S(2)}) copy-start(pred[2,128]{1,0:T(4,128)(4,1)S(1)} %get-tuple-element.106) | copy-start | bytes 772
  24.6 51.9 %copy-start.130 = (pred[2,128]{1,0:T(4,128)(4,1)}, pred[2,128]{1,0:T(4,128)(4,1)S(1)}, u32[]{:S(2)}) copy-start(pred[2,128]{1,0:T(4,128)(4,1)S(1)} %get-tuple-element.107) | copy-start | bytes 772
  24.6 73.2 %copy-start.105 = (f32[1024,1]{0,1:T(1,128)}, f32[1024,1]{0,1:T(1,128)S(1)}, u32[]{:S(2)}) copy-start(f32[1024,1]{0,1:T(1,128)S(1)} %get-tuple-element.129) | copy-start | bytes 12292
  24.6 51.8 %copy-start.15 = (f32[1024,1]{0,1:T(1,128)}, f32[1024,1]{0,1:T(1,128)S(1)}, u32[]{:S(2)}) copy-start(f32[1024,1]{0,1:T(1,128)S(1)} %get-tuple-element.92) | copy-start | bytes 12292
  24.7 51.8 %copy-start.17 = (f32[1024,1]{0,1:T(1,128)}, f32[1024,1]{0,1:T(1,128)S(1)}, u32[]{:S(2)}) copy-start(f32[1024,1]{0,1:T(1,128)S(1)} %get-tuple-element.93) | copy-start | bytes 12292
  24.7 51.8 %copy-start.19 = (f32[1024,1]{0,1:T(1,128)}, f32[1024,1]{0,1:T(1,128)S(1)}, u32[]{:S(2)}) copy-start(f32[1024,1]{0,1:T(1,128)S(1)} %get-tuple-element.94) | copy-start | bytes 12292
  24.7 51.8 %copy-start.21 = (f32[1024,1]{0,1:T(1,128)}, f32[1024,1]{0,1:T(1,128)S(1)}, u32[]{:S(2)}) copy-start(f32[1024,1]{0,1:T(1,128)S(1)} %get-tuple-element.95) | copy-start | bytes 12292
  24.7 51.8 %copy-start.23 = (f32[1024,1]{0,1:T(1,128)}, f32[1024,1]{0,1:T(1,128)S(1)}, u32[]{:S(2)}) copy-start(f32[1024,1]{0,1:T(1,128)S(1)} %get-tuple-element.96) | copy-start | bytes 12292
  24.7 51.8 %copy-start.25 = (f32[1024,1]{0,1:T(1,128)}, f32[1024,1]{0,1:T(1,128)S(1)}, u32[]{:S(2)}) copy-start(f32[1024,1]{0,1:T(1,128)S(1)} %get-tuple-element.97) | copy-start | bytes 12292
  24.7 51.8 %copy-start.27 = (f32[1024,1]{0,1:T(1,128)}, f32[1024,1]{0,1:T(1,128)S(1)}, u32[]{:S(2)}) copy-start(f32[1024,1]{0,1:T(1,128)S(1)} %get-tuple-element.98) | copy-start | bytes 12292
  24.7 51.8 %copy-start.29 = (f32[1024,1]{0,1:T(1,128)}, f32[1024,1]{0,1:T(1,128)S(1)}, u32[]{:S(2)}) copy-start(f32[1024,1]{0,1:T(1,128)S(1)} %get-tuple-element.99) | copy-start | bytes 12292
  24.8 51.7 %copy-start.31 = (f32[1024,1]{0,1:T(1,128)}, f32[1024,1]{0,1:T(1,128)S(1)}, u32[]{:S(2)}) copy-start(f32[1024,1]{0,1:T(1,128)S(1)} %get-tuple-element.69) | copy-start | bytes 12292
  24.8 51.7 %copy-start.33 = (f32[1024,1]{0,1:T(1,128)}, f32[1024,1]{0,1:T(1,128)S(1)}, u32[]{:S(2)}) copy-start(f32[1024,1]{0,1:T(1,128)S(1)} %get-tuple-element.70) | copy-start | bytes 12292
  24.8 51.7 %copy-start.35 = (f32[1024,1]{0,1:T(1,128)}, f32[1024,1]{0,1:T(1,128)S(1)}, u32[]{:S(2)}) copy-start(f32[1024,1]{0,1:T(1,128)S(1)} %get-tuple-element.71) | copy-start | bytes 12292
  24.8 51.7 %copy-start.37 = (f32[1024,1]{0,1:T(1,128)}, f32[1024,1]{0,1:T(1,128)S(1)}, u32[]{:S(2)}) copy-start(f32[1024,1]{0,1:T(1,128)S(1)} %get-tuple-element.72) | copy-start | bytes 12292
  24.8 51.7 %copy-start.39 = (f32[1024,1]{0,1:T(1,128)}, f32[1024,1]{0,1:T(1,128)S(1)}, u32[]{:S(2)}) copy-start(f32[1024,1]{0,1:T(1,128)S(1)} %get-tuple-element.73) | copy-start | bytes 12292
  24.8 51.7 %copy-start.41 = (f32[1024,1]{0,1:T(1,128)}, f32[1024,1]{0,1:T(1,128)S(1)}, u32[]{:S(2)}) copy-start(f32[1024,1]{0,1:T(1,128)S(1)} %get-tuple-element.74) | copy-start | bytes 12292
  24.9 51.7 %copy-start.43 = (f32[1024,1]{0,1:T(1,128)}, f32[1024,1]{0,1:T(1,128)S(1)}, u32[]{:S(2)}) copy-start(f32[1024,1]{0,1:T(1,128)S(1)} %get-tuple-element.75) | copy-start | bytes 12292
  24.9 51.7 %copy-start.45 = (f32[1024,1]{0,1:T(1,128)}, f32[1024,1]{0,1:T(1,128)S(1)}, u32[]{:S(2)}) copy-start(f32[1024,1]{0,1:T(1,128)S(1)} %get-tuple-element.76) | copy-start | bytes 12292
  24.9 51.7 %copy-start.47 = (f32[1024,1]{0,1:T(1,128)}, f32[1024,1]{0,1:T(1,128)S(1)}, u32[]{:S(2)}) copy-start(f32[1024,1]{0,1:T(1,128)S(1)} %get-tuple-element.77) | copy-start | bytes 12292
  24.9 51.7 %copy-start.49 = (f32[1024,1]{0,1:T(1,128)}, f32[1024,1]{0,1:T(1,128)S(1)}, u32[]{:S(2)}) copy-start(f32[1024,1]{0,1:T(1,128)S(1)} %get-tuple-element.78) | copy-start | bytes 12292
  24.9 51.7 %copy-start.51 = (f32[1024,1]{0,1:T(1,128)}, f32[1024,1]{0,1:T(1,128)S(1)}, u32[]{:S(2)}) copy-start(f32[1024,1]{0,1:T(1,128)S(1)} %get-tuple-element.79) | copy-start | bytes 12292
  24.9 51.7 %copy-start.53 = (f32[1024,1]{0,1:T(1,128)}, f32[1024,1]{0,1:T(1,128)S(1)}, u32[]{:S(2)}) copy-start(f32[1024,1]{0,1:T(1,128)S(1)} %get-tuple-element.80) | copy-start | bytes 12292
  24.9 51.7 %copy-start.55 = (f32[1024,1]{0,1:T(1,128)}, f32[1024,1]{0,1:T(1,128)S(1)}, u32[]{:S(2)}) copy-start(f32[1024,1]{0,1:T(1,128)S(1)} %get-tuple-element.81) | copy-start | bytes 12292
  24.9 51.7 %copy-start.57 = (f32[1024,1]{0,1:T(1,128)}, f32[1024,1]{0,1:T(1,128)S(1)}, u32[]{:S(2)}) copy-start(f32[1024,1]{0,1:T(1,128)S(1)} %get-tuple-element.82) | copy-start | bytes 12292
  24.9 51.7 %copy-start.59 = (f32[1024,1]{0,1:T(1,128)}, f32[1024,1]{0,1:T(1,128)S(1)}, u32[]{:S(2)}) copy-start(f32[1024,1]{0,1:T(1,128)S(1)} %get-tuple-element.83) | copy-start | bytes 12292
  24.9 51.7 %copy-start.61 = (f32[1024,1]{0,1:T(1,128)}, f32[1024,1]{0,1:T(1,128)S(1)}, u32[]{:S(2)}) copy-start(f32[1024,1]{0,1:T(1,128)S(1)} %get-tuple-element.84) | copy-start | bytes 12292
  25.0 51.7 %copy-start.63 = (f32[1024,1]{0,1:T(1,128)}, f32[1024,1]{0,1:T(1,128)S(1)}, u32[]{:S(2)}) copy-start(f32[1024,1]{0,1:T(1,128)S(1)} %get-tuple-element.85) | copy-start | bytes 12292
  25.0 51.7 %copy-start.65 = (f32[1024,1]{0,1:T(1,128)}, f32[1024,1]{0,1:T(1,128)S(1)}, u32[]{:S(2)}) copy-start(f32[1024,1]{0,1:T(1,128)S(1)} %get-tuple-element.86) | copy-start | bytes 12292
  25.0 51.7 %copy-start.67 = (f32[1024,1]{0,1:T(1,128)}, f32[1024,1]{0,1:T(1,128)S(1)}, u32[]{:S(2)}) copy-start(f32[1024,1]{0,1:T(1,128)S(1)} %get-tuple-element.87) | copy-start | bytes 12292
  50.2 26.2 %collective-permute-start = (bf16[2,15,1024]{1,2,0:T(8,128)(2,1)S(1)}, bf16[2,15,1024]{1,2,0:T(8,128)(2,1)S(1)}, u32[]{:S(2)}, u32[]{:S(2)}) collective-permute-start(bf16[2,15,1024]{1,2,0:T(8,128)(2,1)S(1)} %get-tuple-element.67), channel_id=1, source_target_pairs={{0,1},{1,2},{2,3},{3,4},{4,5},{5,6},{6,7},{7,8},{8,9},{9,10},{10,1... | collective-permute-start | bytes 184328 | tf_op jit(solution)/shard_map/ppermute | solution.py:14
  53.3 23.1 %collective-permute-start.1 = (bf16[2,15,1024]{1,2,0:T(8,128)(2,1)S(1)}, bf16[2,15,1024]{1,2,0:T(8,128)(2,1)S(1)}, u32[]{:S(2)}, u32[]{:S(2)}) collective-permute-start(bf16[2,15,1024]{1,2,0:T(8,128)(2,1)S(1)} %get-tuple-element.68), channel_id=1, source_target_pairs={{1,0},{2,1},{3,2},{4,3},{5,4},{6,5},{7,6},{8,7},{9,8},{10,9},{11,1... | collective-permute-start | bytes 184328 | tf_op jit(solution)/shard_map/ppermute | solution.py:17
  103.1 31.6 %collective-permute-start.3 = (f32[2,15,1024]{2,0,1:T(2,128)S(1)}, f32[2,15,1024]{2,0,1:T(2,128)S(1)}, u32[]{:S(2)}, u32[]{:S(2)}) collective-permute-start(f32[2,15,1024]{2,0,1:T(2,128)S(1)} %copy.193), channel_id=1, source_target_pairs={{0,1},{1,2},{2,3},{3,4},{4,5},{5,6},{6,7},{7,8},{8,9},{9,10},{10,1... | collective-permute-start | bytes 368648 | tf_op jit(solution)/shard_map/ppermute | solution.py:14
  107.9 26.4 %collective-permute-start.2 = (f32[2,15,1024]{2,0,1:T(2,128)S(1)}, f32[2,15,1024]{2,0,1:T(2,128)S(1)}, u32[]{:S(2)}, u32[]{:S(2)}) collective-permute-start(f32[2,15,1024]{2,0,1:T(2,128)S(1)} %copy.192), channel_id=1, source_target_pairs={{1,0},{2,1},{3,2},{4,3},{5,4},{6,5},{7,6},{8,7},{9,8},{10,9},{11,1... | collective-permute-start | bytes 368648 | tf_op jit(solution)/shard_map/ppermute | solution.py:17
  171.6 21.0 %reduce-scatter.11.cloned.1.call-start = ((), (), s32[]{:S(2)}) async-start(), calls=%async_computation.9 | async-start | bytes 196608 | tf_op jit(solution)/shard_map/reduce_scatter | solution.py:144
  174.7 33.8 %reduce-scatter.9.cloned.1.call-start = ((), (), s32[]{:S(2)}) async-start(), calls=%async_computation.8 | async-start | bytes 6291456 | tf_op jit(solution)/shard_map/reduce_scatter | solution.py:143
  178.7 49.7 %reduce-scatter.7.cloned.1.call-start = ((), (), s32[]{:S(2)}) async-start(), calls=%async_computation.7 | async-start | bytes 12582912 | tf_op jit(solution)/shard_map/reduce_scatter | solution.py:142
  184.5 152.0 %all-reduce.6.cloned.1.call-start = ((), (), s32[]{:S(2)}) async-start(), calls=%async_computation.11 | async-start | bytes 139264 | tf_op jit(solution)/shard_map/psum | solution.py:147
  192.6 362.9 %all-reduce.8.cloned.1.call-start = ((), (), s32[]{:S(2)}) async-start(), calls=%async_computation.12 | async-start | bytes 12582912 | tf_op jit(solution)/shard_map/psum | solution.py:147
  (112 other events, 650.5 us)
Sparse Core Ops, SparseCore 0:
  9.5 15.4 all-gather.2
  26.6 11.7 all-gather.4
  171.8 10.0 reduce-scatter.12
  183.9 8.6 reduce-scatter.10
  195.3 13.1 reduce-scatter.8
  210.7 17.6 reduce-scatter.6
  234.4 101.9 all-reduce.5
  342.7 212.7 all-reduce.7
where the time goes:
time: 573 us; the launch traced here: 569 us
  waiting for transfers between devices  401 us (70%)
  other arithmetic  86.4 us (15%)
  local copies, waits for them, and re-layouts  22.3 us (4%)
  matrix products  20.8 us (4%)
  starting transfers between devices  18.7 us (3%)
  between operations  16.4 us (3%)
    psum x2, waiting for transfers between devices, per_device(): totals = lax.psum((shares[0], shares[1], shares[2], shares[3]), 'seq')  319 us
    add x1, other arithmetic, per_device(): grad_gated + jnp.where(back_same, grad_pad[:, mirror:mirror + frames_dev]...  26.6 us
    reduce_sum x6, other arithmetic, per_device(): jnp.sum(jnp.where(same, grad_cells * gated_pad[:, tap_index:tap_index + f...  24.8 us
    ppermute x2, waiting for transfers between devices, padded(): lax.ppermute(lax.slice_in_dim(block, block.shape[dim] - width, None, axis...  20.1 us
    reduce_scatter x1, waiting for transfers between devices, per_device(): lax.psum_scatter(grad_in_w, 'dp', scatter_dimension=0, tiled=True)  19.9 us
    all_to_all x1, waiting for transfers between devices, per_device(): lax.all_to_all(outgoing, ('dp', 'seq'), split_axis=0, concat_axis=0, tile...  18 us
    reduce_scatter x1, waiting for transfers between devices, per_device(): lax.psum_scatter(grad_out_w, 'dp', scatter_dimension=0, tiled=True)  15.8 us
    reduce_sum x2, other arithmetic, norm_rows(): average = jnp.mean(values, axis=-1, keepdims=True)  15.7 us
  transfers between devices with their start and end apart: 13, of which 7 were waited for; matrix products, arithmetic and copies ran while one was open for 13% of the time, Pallas kernels for 0%

commit v1 on v0

--- a/solution.py
+++ b/solution.py
@@ -1,9 +1,167 @@
+import functools
 import math
 
 import jax
 import jax.numpy as jnp
 from jax import lax
+from jax.experimental import pallas as pl
+from jax.experimental.pallas import tpu as pltpu
 from jax.sharding import PartitionSpec as P
+
+MESH = pl.DeviceIdType.MESH
+
+
+def greet(p, q, n_dp, n_seq):
+    barrier = pltpu.get_barrier_semaphore()
+
+    @pl.loop(1, n_dp)
+    def _(e):
+        pl.semaphore_signal(
+            barrier, inc=1, device_id=(lax.rem(p + e, n_dp), q), device_id_type=MESH
+        )
+
+    @pl.loop(1, n_seq)
+    def _(d):
+        pl.semaphore_signal(
+            barrier, inc=1, device_id=(p, lax.rem(q + d, n_seq)), device_id_type=MESH
+        )
+
+    pl.semaphore_wait(barrier, n_dp + n_seq - 2)
+
+
+def reduce_kernel(n_dp, n_seq, count, *refs):
+    ins, outs, rest = refs[:count], refs[count : 2 * count], refs[2 * count :]
+    own, peer, staged, inbox, final = (rest[i * count : (i + 1) * count] for i in range(5))
+    load_sem, dp_send, dp_recv, rs_send, rs_recv, ag_send, ag_recv, keep_sem = rest[5 * count :]
+    p, q = lax.axis_index("dp"), lax.axis_index("seq")
+    greet(p, q, n_dp, n_seq)
+
+    def to_dp(a, e, d):
+        other = lax.rem(p + e, n_dp)
+        return pltpu.make_async_remote_copy(
+            src_ref=ins[a].at[other, lax.rem(q + d, n_seq)],
+            dst_ref=peer[a].at[e - 1, d],
+            send_sem=dp_send.at[a, e - 1, d],
+            recv_sem=dp_recv.at[a, e - 1, d],
+            device_id=(other, q),
+            device_id_type=MESH,
+        )
+
+    def to_own(a, d):
+        return pltpu.make_async_copy(
+            ins[a].at[p, lax.rem(q + d, n_seq)], own[a].at[d], load_sem.at[a, d]
+        )
+
+    def to_seq(a, d):
+        return pltpu.make_async_remote_copy(
+            src_ref=staged[a].at[d],
+            dst_ref=inbox[a].at[d],
+            send_sem=rs_send.at[a, d],
+            recv_sem=rs_recv.at[a, d],
+            device_id=(p, lax.rem(q + d, n_seq)),
+            device_id_type=MESH,
+        )
+
+    def to_all(a, d):
+        return pltpu.make_async_remote_copy(
+            src_ref=final[a],
+            dst_ref=outs[a].at[q],
+            send_sem=ag_send.at[a, d],
+            recv_sem=ag_recv.at[a, d],
+            device_id=(p, lax.rem(q + d, n_seq)),
+            device_id_type=MESH,
+        )
+
+    @pl.loop(0, n_seq)
+    def _(step):
+        d = lax.rem(step + 1, n_seq)
+        for a in range(count):
+            to_own(a, d).start()
+
+            @pl.loop(1, n_dp)
+            def _(e):
+                to_dp(a, e, d).start()
+
+    def dp_sum(a, d):
+        to_own(a, d).wait()
+        total = own[a][d].astype(jnp.float32)
+        for e in range(1, n_dp):
+            to_dp(a, e, d).wait_recv()
+            total = total + peer[a][e - 1, d].astype(jnp.float32)
+        return total
+
+    @pl.loop(1, n_seq)
+    def _(d):
+        for a in range(count):
+            staged[a][d] = dp_sum(a, d).astype(staged[a].dtype)
+            to_seq(a, d).start()
+
+    for a in range(count):
+        total = dp_sum(a, 0)
+
+        def gather(d, value):
+            to_seq(a, d).wait_recv()
+            return value + inbox[a][d].astype(jnp.float32)
+
+        total = lax.fori_loop(1, n_seq, gather, total)
+        final[a][...] = total.astype(final[a].dtype)
+
+        @pl.loop(1, n_seq)
+        def _(d):
+            to_all(a, d).start()
+
+        pltpu.make_async_copy(final[a], outs[a].at[q], keep_sem.at[a]).start()
+
+    @pl.loop(1, n_seq)
+    def _(d):
+        for a in range(count):
+            to_seq(a, d).wait_send()
+            to_all(a, d).wait_send()
+            to_all(a, d).wait_recv()
+
+    for a in range(count):
+        pltpu.make_async_copy(final[a], outs[a].at[q], keep_sem.at[a]).wait()
+
+        @pl.loop(0, n_seq)
+        def _(d):
+            @pl.loop(1, n_dp)
+            def _(e):
+                to_dp(a, e, d).wait_send()
+
+
+def reduce_all(parts):
+    n_dp, n_seq = lax.axis_size("dp"), lax.axis_size("seq")
+    count = len(parts)
+    dma = pltpu.SemaphoreType.DMA
+    vmem = pltpu.VMEM
+    tiles = [part.shape[2:] for part in parts]
+    kinds = [part.dtype for part in parts]
+    pairs = list(zip(tiles, kinds))
+    return pl.pallas_call(
+        functools.partial(reduce_kernel, n_dp, n_seq, count),
+        out_shape=[jax.ShapeDtypeStruct((n_seq, *tile), kind) for tile, kind in pairs],
+        in_specs=[pl.BlockSpec(memory_space=pl.ANY)] * count,
+        out_specs=[pl.BlockSpec(memory_space=pl.ANY)] * count,
+        scratch_shapes=(
+            [vmem((n_seq, *tile), kind) for tile, kind in pairs]
+            + [vmem((n_dp - 1, n_seq, *tile), kind) for tile, kind in pairs]
+            + [vmem((n_seq, *tile), kind) for tile, kind in pairs]
+            + [vmem((n_seq, *tile), kind) for tile, kind in pairs]
+            + [vmem(tile, kind) for tile, kind in pairs]
+            + [
+                dma((count, n_seq)),
+                dma((count, n_dp - 1, n_seq)),
+                dma((count, n_dp - 1, n_seq)),
+                dma((count, n_seq)),
+                dma((count, n_seq)),
+                dma((count, n_seq)),
+                dma((count, n_seq)),
+                dma((count,)),
+            ]
+        ),
+        compiler_params=pltpu.CompilerParams(collective_id=0, has_side_effects=True),
+        name="reduce_all",
+    )(*parts)
 
 
 def padded(block, sides, width):
@@ -137,22 +295,31 @@
         .astype(jnp.bfloat16)
         .reshape(slabs, frames_dev, width)
     )
-    grad_gain = jnp.stack([grad_gain_pre, grad_gain_mid], axis=1)
-    shares = (
-        lax.psum_scatter(grad_in_w, "dp", scatter_dimension=0, tiled=True),
-        lax.psum_scatter(grad_out_w, "dp", scatter_dimension=0, tiled=True),
-        lax.psum_scatter(grad_taps, "dp", scatter_dimension=0, tiled=True),
-        lax.psum_scatter(grad_gain, "dp", scatter_dimension=0, tiled=True),
-    )
-    totals = lax.psum((shares[0], shares[1], shares[2], shares[3]), "seq")
-    scale = 1.0 / math.sqrt(lax.axis_size("dp") * lax.axis_size("seq") * rows_dev)
+    n_dp, n_seq = lax.axis_size("dp"), lax.axis_size("seq")
+    held = width // n_dp
+    piece = held // n_seq
+    smalls = jnp.concatenate([grad_taps.T, grad_gain_pre[None], grad_gain_mid[None]], axis=0)
+    lines = smalls.shape[0]
+    per_dev = lines * held // n_seq
+    small_rows = -(-per_dev // 1024) * 8
+    smalls = smalls.reshape(lines, n_dp, held).transpose(1, 0, 2).reshape(n_dp, n_seq, per_dev)
+    smalls = jnp.pad(smalls, ((0, 0), (0, 0), (0, small_rows * 128 - per_dev)))
+    sum_in, sum_out, sum_small = reduce_all(
+        (
+            grad_in_w.astype(jnp.bfloat16).reshape(n_dp, n_seq, piece, 2 * width),
+            grad_out_w.astype(jnp.bfloat16).reshape(n_dp, n_seq, piece, width),
+            smalls.reshape(n_dp, n_seq, small_rows, 128),
+        )
+    )
+    scale = 1.0 / math.sqrt(n_dp * n_seq * rows_dev)
+    small = sum_small.reshape(n_seq, -1)[:, :per_dev].reshape(lines, held).T * scale
     return (
         encoded,
         grad_frames,
-        totals[0] * scale,
-        totals[1] * scale,
-        totals[2] * scale,
-        totals[3] * scale,
+        sum_in.reshape(held, 2 * width).astype(jnp.float32) * scale,
+        sum_out.reshape(held, width).astype(jnp.float32) * scale,
+        small[:, :kernel_len],
+        small[:, kernel_len:],
     )
 
 

time: 573 us -> 373 us (0.65)
  waiting for transfers between devices: 401 us -> 39.5 us
  Pallas kernels: 0 us -> 174 us
    psum x2 -> x0, waiting for transfers between devices: 319 us -> none  [per_device(): totals = lax.psum((shares[0], shares[1], shares[2], shares[3]), 'seq')]
    pallas_call x0 -> x1, Pallas kernels: none -> 174 us  [reduce_all(): pl.pallas_call(functools.partial(reduce_kernel, n_dp, n_seq, count), out_...]
    reduce_scatter x3 -> x0, waiting for transfers between devices: 42.1 us -> none  [the longest x1 19.9 us: per_device(): lax.psum_scatter(grad_in_w, 'dp', scatter_dimension=0, tiled=True)]
  transfers between devices with their start and end apart: 13 -> 7, of which waited for: 7 -> 2; matrix products, arithmetic and copies ran while one was open for 13% -> 15% of each run, Pallas kernels for 0% -> 0%
where the time goes in v1:
time: 373 us; the launch traced here: 371 us
  Pallas kernels  174 us (47%)
  other arithmetic  82.1 us (22%)
  waiting for transfers between devices  39.5 us (11%)
  local copies, waits for them, and re-layouts  20.4 us (5%)
  starting transfers between devices  18.4 us (5%)
  matrix products  17.5 us (5%)
  between operations  15.4 us (4%)
  blocking collectives  3.78 us (1%)
    pallas_call x1, Pallas kernels, reduce_all(): pl.pallas_call(functools.partial(reduce_kernel, n_dp, n_seq, count), out_...  174 us
    add x1, other arithmetic, per_device(): grad_gated + jnp.where(back_same, grad_pad[:, mirror:mirror + frames_dev]...  28.7 us
    reduce_sum x6, other arithmetic, per_device(): jnp.sum(jnp.where(same, grad_cells * gated_pad[:, tap_index:tap_index + f...  22.2 us
    ppermute x2, waiting for transfers between devices, padded(): lax.ppermute(lax.slice_in_dim(block, block.shape[dim] - width, None, axis...  20.1 us
    all_to_all x1, waiting for transfers between devices, per_device(): lax.all_to_all(outgoing, ('dp', 'seq'), split_axis=0, concat_axis=0, tile...  18 us
    reduce_sum x2, other arithmetic, norm_rows(): average = jnp.mean(values, axis=-1, keepdims=True)  15.4 us
  transfers between devices with their start and end apart: 7, of which 2 were waited for; matrix products, arithmetic and copies ran while one was open for 15% of the time, Pallas kernels for 0%

profile of v1, /device:TPU:19, one launch (start us, length us, event | category | flops | bytes accessed | tf_op | source)
XLA Modules:
  0.0 371.2 jit_solution(13044603809864171934)
XLA Ops:
  7.2 0.7 all-gather.3.cloned.1.call-update
  8.4 2.1 gather_fusion
  10.6 1.2 select_select_fusion
  11.8 6.2 %all-to-all-start = ((bf16[32,16,1024]{2,1,0:T(8,128)(2,1)}), bf16[32,16,1024]{2,1,0:T(8,128)(2,1)S(1)}, u32[]{:S(2)}, u32[]{:S(2)}) async-start(bf16[32,16,1024]{2,1,0:T(8,128)(2,1)} %select_select_fusion), calls=%async_computation | async-start | bytes 2097152 | tf_op jit(solution)/shard_map/all_to_all | solution.py:212
  18.0 0.7 all-gather.5.cloned.1.call-update
  19.1 1.9 all_gather.12
  21.0 1.9 all_gather.14
  22.9 0.7 fusion.294
  23.7 0.8 fusion.295
  24.9 18.0 %all-to-all-done = bf16[32,16,1024]{2,1,0:T(8,128)(2,1)S(1)} async-done(((bf16[32,16,1024]{2,1,0:T(8,128)(2,1)}), bf16[32,16,1024]{2,1,0:T(8,128)(2,1)S(1)}, u32[]{:S(2)}, u32[]{:S(2)}) %all-to-all-start) | async-done | bytes 1048608 | tf_op jit(solution)/shard_map/all_to_all | solution.py:212
  43.0 1.2 gather_fusion.1
  44.8 3.6 fusion.331
  48.7 1.0 copy-done.1
  50.2 3.0 collective-permute-start
  53.3 2.2 collective-permute-start.1
  55.5 0.7 fusion.296
  56.3 20.1 %collective-permute-done = bf16[2,15,1024]{1,2,0:T(8,128)(2,1)S(1)} collective-permute-done((bf16[2,15,1024]{1,2,0:T(8,128)(2,1)S(1)}, bf16[2,15,1024]{1,2,0:T(8,128)(2,1)S(1)}, u32[]{:S(2)}, u32[]{:S(2)}) %collective-permute-start) | collective-permute-done | bytes 61472 | tf_op jit(solution)/shard_map/ppermute | solution.py:172
  77.2 15.2 %fusion.336 = (f32[2,128]{1,0:T(2,128)S(1)}, f32[2,128,1024]{1,2,0:T(8,128)S(1)}) fusion(f32[1024]{0:T(1024)S(1)} %bitcast.187, bf16[2,15,1024]{1,2,0:T(8,128)(2,1)S(1)} %collective-permute-done.1, bf16[2,128,1024]{1,2,0:T(8,128)(2,1)S(1)} %copy.148, pred[2,128]{1,0:T(4,128)(4,1)} %get-tuple-element.130, f32[1024]{0:T(1024)S(1)} %bitcast.185, ...), kind=kLoop, calls=%fused_computation.600 | loop fusion | flops 55836416 | bytes 1831424 | tf_op jit(solution)/shard_map/jvp()/reduce_sum | solution.py:181
  92.4 1.3 copy.153
  94.0 4.0 %multiply_reduce_fusion = (f32[1024]{0:T(1024)}, f32[256]{0:T(256)S(1)}, f32[256,1024]{1,0:T(8,128)S(1)}) fusion(f32[2,128,1024]{2,1,0:T(8,128)} %copy.153, f32[256]{0:T(256)S(1)} %bitcast_rsqrt_fusion, f32[256]{0:T(256)S(1)} %get-tuple-element.133, f32[1024]{0:T(1024)S(1)} %bitcast.257, bf16[256,1024]{1,0:T(8,128)(2,1)} %bitcast.154, ...), kind=kOutput, calls=%fused_computation.449 | convolution fusion | flops 541326080 | bytes 4729856 | tf_op jit(solution)/shard_map/dot_general | solution.py:259
  98.0 1.4 fusion.334
  99.5 1.3 multiply_reduce_fusion.1
  100.8 1.5 copy.155
  102.4 1.0 fusion.341
  103.5 3.0 collective-permute-start.2
  106.5 0.7 copy.194
  107.3 3.8 %collective-permute-start.3 = (f32[2,15,1024]{2,0,1:T(2,128)}, f32[2,15,1024]{2,0,1:T(2,128)}, u32[]{:S(2)}, u32[]{:S(2)}) collective-permute-start(f32[2,15,1024]{2,0,1:T(2,128)} %copy.194), channel_id=1, source_target_pairs={{0,1},{1,2},{2,3},{3,4},{4,5},{5,6},{6,7},{7,8},{8,9},{9,10},{10,1... | collective-permute-start | bytes 368648 | tf_op jit(solution)/shard_map/ppermute | solution.py:172
  111.1 3.5 bitcast_convert_fusion
  114.8 4.3 %fusion.128 = (f32[1024]{0:T(1024)S(1)}, f32[1024]{0:T(1024)S(1)}, f32[1024]{0:T(1024)S(1)}, f32[1024]{0:T(1024)S(1)}, f32[1024]{0:T(1024)S(1)}, /*index=5*/f32[1024]{0:T(1024)S(1)}) fusion(f32[2,128,1024]{1,2,0:T(8,128)S(1)} %copy.155, pred[2,128]{1,0:T(4,128)(4,1)} %get-tuple-element.130, bf16[2,15,1024]{1,2,0:T(8,128)(2,1)S(1)} %copy-done.6, ...), kind=kLoop, calls=%fused_computation.312 | loop fusion | flops 11003904 | bytes 1660416 | tf_op jit(solution)/shard_map/reduce_sum | solution.py:270
  119.1 4.1 %fusion.125 = (f32[1024]{0:T(1024)S(1)}, f32[1024]{0:T(1024)S(1)}, f32[1024]{0:T(1024)S(1)}, f32[1024]{0:T(1024)S(1)}, f32[1024]{0:T(1024)S(1)}, /*index=5*/f32[1024]{0:T(1024)S(1)}) fusion(f32[2,128,1024]{1,2,0:T(8,128)S(1)} %copy.155, pred[2,128]{1,0:T(4,128)(4,1)S(1)} %get-tuple-element.103, bf16[2,15,1024]{1,2,0:T(8,128)(2,1)S(1)} %copy-done.6, ...), kind=kLoop, calls=%fused_computation.309 | loop fusion | flops 11003904 | bytes 1660416 | tf_op jit(solution)/shard_map/reduce_sum | solution.py:270
  123.3 4.2 %fusion.77 = (f32[1024]{0:T(1024)S(1)}, f32[1024]{0:T(1024)S(1)}, f32[1024]{0:T(1024)S(1)}, f32[1024]{0:T(1024)S(1)}, f32[1024]{0:T(1024)S(1)}, /*index=5*/f32[1024]{0:T(1024)S(1)}) fusion(f32[2,128,1024]{1,2,0:T(8,128)S(1)} %copy.155, pred[2,128]{1,0:T(4,128)(4,1)} %get-tuple-element.117, bf16[2,128,1024]{1,2,0:T(8,128)(2,1)S(1)} %copy.148, ...), kind=kLoop, calls=%fused_computation.261 | loop fusion | flops 11003904 | bytes 1660416 | tf_op jit(solution)/shard_map/reduce_sum | solution.py:270
  127.5 4.4 %fusion.59 = (f32[1024]{0:T(1024)S(1)}, f32[1024]{0:T(1024)S(1)}, f32[1024]{0:T(1024)S(1)}, f32[1024]{0:T(1024)S(1)}, f32[1024]{0:T(1024)S(1)}, /*index=5*/f32[1024]{0:T(1024)S(1)}) fusion(f32[2,128,1024]{1,2,0:T(8,128)S(1)} %copy.155, pred[2,128]{1,0:T(4,128)(4,1)} %get-tuple-element.124, bf16[2,128,1024]{1,2,0:T(8,128)(2,1)S(1)} %copy.148, ...), kind=kLoop, calls=%fused_computation.243 | loop fusion | flops 11003904 | bytes 1660416 | tf_op jit(solution)/shard_map/reduce_sum | solution.py:270
  131.9 4.0 %fusion.86 = (f32[1024]{0:T(1024)S(1)}, f32[1024]{0:T(1024)S(1)}, f32[1024]{0:T(1024)S(1)}, f32[1024]{0:T(1024)S(1)}, f32[1024]{0:T(1024)S(1)}, /*index=5*/f32[1024]{0:T(1024)S(1)}) fusion(f32[2,128,1024]{1,2,0:T(8,128)S(1)} %copy.155, pred[2,128]{1,0:T(4,128)(4,1)} %get-tuple-element.114, bf16[2,15,1024]{1,2,0:T(8,128)(2,1)S(1)} %copy-done.6, ...), kind=kLoop, calls=%fused_computation.270 | loop fusion | flops 11003904 | bytes 1721856 | tf_op jit(solution)/shard_map/reduce_sum | solution.py:270
  135.9 1.5 fusion.4
  137.8 0.6 concatenate.91
  138.8 2.2 copy.159
  141.1 28.7 %fusion.137 = f32[2,128,1024]{1,2,0:T(8,128)} fusion(f32[2,15,1024]{1,2,0:T(8,128)} %copy.159, f32[2,128,1024]{1,2,0:T(8,128)S(1)} %copy.155, f32[2,15,1024]{1,2,0:T(8,128)S(1)} %copy.156, f32[1024]{0:T(1024)} %bitcast.188, f32[1024]{0:T(1024)} %bitcast.186, f32[1024]{0:T(1024)} %bitcast.184, f32[1024]{0:T(1024)} %bitcast.182, f32[1024]{0:T(1024)S(1)} %bitcast.180, ...), kind=kLoop, calls=%fused_computation.321 | loop fusion | flops 31719424 | bytes 2477568 | tf_op jit(solution)/shard_map/add | solution.py:282
  169.8 2.7 copy.161
  172.5 1.7 fusion.254
  174.3 3.5 convolution_convert_fusion
  177.8 1.4 fusion.130
  180.1 0.8 copy.195
  180.9 174.0 %reduce_all.1 = (bf16[16,32,2048]{2,1,0:T(8,128)(2,1)}, bf16[16,32,1024]{2,1,0:T(8,128)(2,1)}, f32[16,16,128]{2,1,0:T(8,128)}) custom-call(bf16[2,16,32,2048]{3,2,1,0:T(8,128)(2,1)} %bitcast.147, bf16[2,16,32,1024]{3,2,1,0:T(8,128)(2,1)} %bitcast.148, f32[2,16,16,128]{3,2,1,0:T(8,128)} %bitcast.151), custom_call_target="tpu_custom_call" | custom-call | tf_op jit(solution)/shard_map/reduce_all/pallas_call | solution.py:140
  354.9 0.9 copy.198
  356.0 0.6 slice.872
  357.2 4.3 %convert_multiply_fusion = f32[16,32,2048]{2,1,0:T(8,128)} fusion(bf16[16,32,2048]{2,1,0:T(8,128)(2,1)} %get-tuple-element.9), kind=kLoop, calls=%fused_computation.59 | loop fusion | flops 2097152 | bytes 6291456 | tf_op jit(solution)/shard_map/mul | solution.py:319
  361.5 1.6 convert_multiply_fusion.1
  363.1 1.3 add_convert_fusion
  (211 shorter events, 6.1 us)
Async XLA Ops:
  7.2 37.6 %all-gather.3.cloned.1.call-start = ((), (), s32[]{:S(2)}) async-start(), calls=%async_computation.1 | async-start | bytes 6291456 | tf_op jit(solution)/shard_map/all_gather | solution.py:233
  11.8 9.2 %copy-start.35 = (bf16[512,31]{0,1:T(8,128)(2,1)S(1)}, bf16[512,31]{0,1:T(8,128)(2,1)}, u32[]{:S(2)}) copy-start(bf16[512,31]{0,1:T(8,128)(2,1)} %param.13) | copy-start | bytes 95236
  11.8 11.1 %copy-start.11 = (s32[2,2048]{1,0:T(2,128)S(1)}, s32[2,2048]{1,0:T(2,128)}, u32[]{:S(2)}) copy-start(s32[2,2048]{1,0:T(2,128)} %param.10) | copy-start | bytes 49156
  11.8 31.2 %all-to-all-start = ((bf16[32,16,1024]{2,1,0:T(8,128)(2,1)}), bf16[32,16,1024]{2,1,0:T(8,128)(2,1)S(1)}, u32[]{:S(2)}, u32[]{:S(2)}) async-start(bf16[32,16,1024]{2,1,0:T(8,128)(2,1)} %select_select_fusion), calls=%async_computation | async-start | bytes 2097152 | tf_op jit(solution)/shard_map/all_to_all | solution.py:212
  18.0 76.0 %all-gather.5.cloned.1.call-start = ((), (), s32[]{:S(2)}) async-start(), calls=%async_computation.2 | async-start | bytes 3145728 | tf_op jit(solution)/shard_map/all_gather | solution.py:234
  23.7 21.1 %copy-start.40 = (pred[256]{0:T(512)(128)(4,1)}, pred[256]{0:T(512)(128)(4,1)S(1)}, u32[]{:S(2)}) copy-start(pred[256]{0:T(512)(128)(4,1)S(1)} %compare_and_fusion.1) | copy-start | bytes 772
  24.5 51.9 %copy-start.48 = (pred[2,128]{1,0:T(4,128)(4,1)}, pred[2,128]{1,0:T(4,128)(4,1)S(1)}, u32[]{:S(2)}) copy-start(pred[2,128]{1,0:T(4,128)(4,1)S(1)} %get-tuple-element.104) | copy-start | bytes 772
  24.5 51.9 %copy-start.50 = (pred[2,128]{1,0:T(4,128)(4,1)}, pred[2,128]{1,0:T(4,128)(4,1)S(1)}, u32[]{:S(2)}) copy-start(pred[2,128]{1,0:T(4,128)(4,1)S(1)} %get-tuple-element.105) | copy-start | bytes 772
  24.5 51.9 %copy-start.52 = (pred[2,128]{1,0:T(4,128)(4,1)}, pred[2,128]{1,0:T(4,128)(4,1)S(1)}, u32[]{:S(2)}) copy-start(pred[2,128]{1,0:T(4,128)(4,1)S(1)} %get-tuple-element.106) | copy-start | bytes 772
  24.5 51.9 %copy-start.54 = (pred[2,128]{1,0:T(4,128)(4,1)}, pred[2,128]{1,0:T(4,128)(4,1)S(1)}, u32[]{:S(2)}) copy-start(pred[2,128]{1,0:T(4,128)(4,1)S(1)} %get-tuple-element.107) | copy-start | bytes 772
  24.5 51.9 %copy-start.56 = (pred[2,128]{1,0:T(4,128)(4,1)}, pred[2,128]{1,0:T(4,128)(4,1)S(1)}, u32[]{:S(2)}) copy-start(pred[2,128]{1,0:T(4,128)(4,1)S(1)} %get-tuple-element.108) | copy-start | bytes 772
  24.5 51.9 %copy-start.58 = (pred[2,128]{1,0:T(4,128)(4,1)}, pred[2,128]{1,0:T(4,128)(4,1)S(1)}, u32[]{:S(2)}) copy-start(pred[2,128]{1,0:T(4,128)(4,1)S(1)} %get-tuple-element.109) | copy-start | bytes 772
  24.5 51.9 %copy-start.60 = (pred[2,128]{1,0:T(4,128)(4,1)}, pred[2,128]{1,0:T(4,128)(4,1)S(1)}, u32[]{:S(2)}) copy-start(pred[2,128]{1,0:T(4,128)(4,1)S(1)} %get-tuple-element.110) | copy-start | bytes 772
  24.5 51.9 %copy-start.62 = (pred[2,128]{1,0:T(4,128)(4,1)}, pred[2,128]{1,0:T(4,128)(4,1)S(1)}, u32[]{:S(2)}) copy-start(pred[2,128]{1,0:T(4,128)(4,1)S(1)} %get-tuple-element.111) | copy-start | bytes 772
  24.6 51.9 %copy-start.64 = (pred[2,128]{1,0:T(4,128)(4,1)}, pred[2,128]{1,0:T(4,128)(4,1)S(1)}, u32[]{:S(2)}) copy-start(pred[2,128]{1,0:T(4,128)(4,1)S(1)} %get-tuple-element.112) | copy-start | bytes 772
  24.6 94.5 %copy-start.47 = (pred[2,128]{1,0:T(4,128)(4,1)}, pred[2,128]{1,0:T(4,128)(4,1)S(1)}, u32[]{:S(2)}) copy-start(pred[2,128]{1,0:T(4,128)(4,1)S(1)} %get-tuple-element.103) | copy-start | bytes 772
  24.6 51.9 %copy-start.12 = (f32[1024,1]{0,1:T(1,128)}, f32[1024,1]{0,1:T(1,128)S(1)}, u32[]{:S(2)}) copy-start(f32[1024,1]{0,1:T(1,128)S(1)} %get-tuple-element.98) | copy-start | bytes 12292
  24.6 51.9 %copy-start.13 = (f32[1024,1]{0,1:T(1,128)}, f32[1024,1]{0,1:T(1,128)S(1)}, u32[]{:S(2)}) copy-start(f32[1024,1]{0,1:T(1,128)S(1)} %get-tuple-element.99) | copy-start | bytes 12292
  24.7 51.9 %copy-start.14 = (f32[1024,1]{0,1:T(1,128)}, f32[1024,1]{0,1:T(1,128)S(1)}, u32[]{:S(2)}) copy-start(f32[1024,1]{0,1:T(1,128)S(1)} %get-tuple-element.100) | copy-start | bytes 12292
  24.7 51.9 %copy-start.15 = (f32[1024,1]{0,1:T(1,128)}, f32[1024,1]{0,1:T(1,128)S(1)}, u32[]{:S(2)}) copy-start(f32[1024,1]{0,1:T(1,128)S(1)} %get-tuple-element.101) | copy-start | bytes 12292
  24.7 51.8 %copy-start.16 = (f32[1024,1]{0,1:T(1,128)}, f32[1024,1]{0,1:T(1,128)S(1)}, u32[]{:S(2)}) copy-start(f32[1024,1]{0,1:T(1,128)S(1)} %get-tuple-element.71) | copy-start | bytes 12292
  24.8 51.8 %copy-start.17 = (f32[1024,1]{0,1:T(1,128)}, f32[1024,1]{0,1:T(1,128)S(1)}, u32[]{:S(2)}) copy-start(f32[1024,1]{0,1:T(1,128)S(1)} %get-tuple-element.72) | copy-start | bytes 12292
  24.8 51.8 %copy-start.18 = (f32[1024,1]{0,1:T(1,128)}, f32[1024,1]{0,1:T(1,128)S(1)}, u32[]{:S(2)}) copy-start(f32[1024,1]{0,1:T(1,128)S(1)} %get-tuple-element.73) | copy-start | bytes 12292
  24.8 51.8 %copy-start.19 = (f32[1024,1]{0,1:T(1,128)}, f32[1024,1]{0,1:T(1,128)S(1)}, u32[]{:S(2)}) copy-start(f32[1024,1]{0,1:T(1,128)S(1)} %get-tuple-element.74) | copy-start | bytes 12292
  24.8 51.8 %copy-start.20 = (f32[1024,1]{0,1:T(1,128)}, f32[1024,1]{0,1:T(1,128)S(1)}, u32[]{:S(2)}) copy-start(f32[1024,1]{0,1:T(1,128)S(1)} %get-tuple-element.75) | copy-start | bytes 12292
  24.8 51.8 %copy-start.21 = (f32[1024,1]{0,1:T(1,128)}, f32[1024,1]{0,1:T(1,128)S(1)}, u32[]{:S(2)}) copy-start(f32[1024,1]{0,1:T(1,128)S(1)} %get-tuple-element.76) | copy-start | bytes 12292
  24.8 51.8 %copy-start.22 = (f32[1024,1]{0,1:T(1,128)}, f32[1024,1]{0,1:T(1,128)S(1)}, u32[]{:S(2)}) copy-start(f32[1024,1]{0,1:T(1,128)S(1)} %get-tuple-element.77) | copy-start | bytes 12292
  24.8 51.8 %copy-start.23 = (f32[1024,1]{0,1:T(1,128)}, f32[1024,1]{0,1:T(1,128)S(1)}, u32[]{:S(2)}) copy-start(f32[1024,1]{0,1:T(1,128)S(1)} %get-tuple-element.78) | copy-start | bytes 12292
  24.8 51.8 %copy-start.24 = (f32[1024,1]{0,1:T(1,128)}, f32[1024,1]{0,1:T(1,128)S(1)}, u32[]{:S(2)}) copy-start(f32[1024,1]{0,1:T(1,128)S(1)} %get-tuple-element.79) | copy-start | bytes 12292
  24.8 51.8 %copy-start.25 = (f32[1024,1]{0,1:T(1,128)}, f32[1024,1]{0,1:T(1,128)S(1)}, u32[]{:S(2)}) copy-start(f32[1024,1]{0,1:T(1,128)S(1)} %get-tuple-element.80) | copy-start | bytes 12292
  24.8 51.8 %copy-start.26 = (f32[1024,1]{0,1:T(1,128)}, f32[1024,1]{0,1:T(1,128)S(1)}, u32[]{:S(2)}) copy-start(f32[1024,1]{0,1:T(1,128)S(1)} %get-tuple-element.81) | copy-start | bytes 12292
  24.9 51.8 %copy-start.27 = (f32[1024,1]{0,1:T(1,128)}, f32[1024,1]{0,1:T(1,128)S(1)}, u32[]{:S(2)}) copy-start(f32[1024,1]{0,1:T(1,128)S(1)} %get-tuple-element.82) | copy-start | bytes 12292
  24.9 51.8 %copy-start.28 = (f32[1024,1]{0,1:T(1,128)}, f32[1024,1]{0,1:T(1,128)S(1)}, u32[]{:S(2)}) copy-start(f32[1024,1]{0,1:T(1,128)S(1)} %get-tuple-element.83) | copy-start | bytes 12292
  24.9 51.8 %copy-start.29 = (f32[1024,1]{0,1:T(1,128)}, f32[1024,1]{0,1:T(1,128)S(1)}, u32[]{:S(2)}) copy-start(f32[1024,1]{0,1:T(1,128)S(1)} %get-tuple-element.84) | copy-start | bytes 12292
  24.9 51.8 %copy-start.30 = (f32[1024,1]{0,1:T(1,128)}, f32[1024,1]{0,1:T(1,128)S(1)}, u32[]{:S(2)}) copy-start(f32[1024,1]{0,1:T(1,128)S(1)} %get-tuple-element.85) | copy-start | bytes 12292
  24.9 51.8 %copy-start.31 = (f32[1024,1]{0,1:T(1,128)}, f32[1024,1]{0,1:T(1,128)S(1)}, u32[]{:S(2)}) copy-start(f32[1024,1]{0,1:T(1,128)S(1)} %get-tuple-element.86) | copy-start | bytes 12292
  24.9 51.8 %copy-start.32 = (f32[1024,1]{0,1:T(1,128)}, f32[1024,1]{0,1:T(1,128)S(1)}, u32[]{:S(2)}) copy-start(f32[1024,1]{0,1:T(1,128)S(1)} %get-tuple-element.87) | copy-start | bytes 12292
  24.9 51.8 %copy-start.33 = (f32[1024,1]{0,1:T(1,128)}, f32[1024,1]{0,1:T(1,128)S(1)}, u32[]{:S(2)}) copy-start(f32[1024,1]{0,1:T(1,128)S(1)} %get-tuple-element.88) | copy-start | bytes 12292
  24.9 51.8 %copy-start.34 = (f32[1024,1]{0,1:T(1,128)}, f32[1024,1]{0,1:T(1,128)S(1)}, u32[]{:S(2)}) copy-start(f32[1024,1]{0,1:T(1,128)S(1)} %get-tuple-element.89) | copy-start | bytes 12292
  50.2 26.2 %collective-permute-start = (bf16[2,15,1024]{1,2,0:T(8,128)(2,1)S(1)}, bf16[2,15,1024]{1,2,0:T(8,128)(2,1)S(1)}, u32[]{:S(2)}, u32[]{:S(2)}) collective-permute-start(bf16[2,15,1024]{1,2,0:T(8,128)(2,1)S(1)} %get-tuple-element.69), channel_id=1, source_target_pairs={{0,1},{1,2},{2,3},{3,4},{4,5},{5,6},{6,7},{7,8},{8,9},{9,10},{10,1... | collective-permute-start | bytes 184328 | tf_op jit(solution)/shard_map/ppermute | solution.py:172
  53.3 23.1 %collective-permute-start.1 = (bf16[2,15,1024]{1,2,0:T(8,128)(2,1)S(1)}, bf16[2,15,1024]{1,2,0:T(8,128)(2,1)S(1)}, u32[]{:S(2)}, u32[]{:S(2)}) collective-permute-start(bf16[2,15,1024]{1,2,0:T(8,128)(2,1)S(1)} %get-tuple-element.70), channel_id=1, source_target_pairs={{1,0},{2,1},{3,2},{4,3},{5,4},{6,5},{7,6},{8,7},{9,8},{10,9},{11,1... | collective-permute-start | bytes 184328 | tf_op jit(solution)/shard_map/ppermute | solution.py:175
  56.3 37.5 %copy-start.66 = (pred[2,128]{1,0:T(4,128)(4,1)}, pred[2,128]{1,0:T(4,128)(4,1)S(1)}, u32[]{:S(2)}) copy-start(pred[2,128]{1,0:T(4,128)(4,1)S(1)} %get-tuple-element.120) | copy-start | bytes 772
  56.3 37.5 %copy-start.68 = (pred[2,128]{1,0:T(4,128)(4,1)}, pred[2,128]{1,0:T(4,128)(4,1)S(1)}, u32[]{:S(2)}) copy-start(pred[2,128]{1,0:T(4,128)(4,1)S(1)} %get-tuple-element.121) | copy-start | bytes 772
  56.3 37.5 %copy-start.70 = (pred[2,128]{1,0:T(4,128)(4,1)}, pred[2,128]{1,0:T(4,128)(4,1)S(1)}, u32[]{:S(2)}) copy-start(pred[2,128]{1,0:T(4,128)(4,1)S(1)} %get-tuple-element.122) | copy-start | bytes 772
  56.3 37.5 %copy-start.72 = (pred[2,128]{1,0:T(4,128)(4,1)}, pred[2,128]{1,0:T(4,128)(4,1)S(1)}, u32[]{:S(2)}) copy-start(pred[2,128]{1,0:T(4,128)(4,1)S(1)} %get-tuple-element.123) | copy-start | bytes 772
  103.5 35.0 %collective-permute-start.2 = (f32[2,15,1024]{2,0,1:T(2,128)S(1)}, f32[2,15,1024]{2,0,1:T(2,128)S(1)}, u32[]{:S(2)}, u32[]{:S(2)}) collective-permute-start(f32[2,15,1024]{2,0,1:T(2,128)S(1)} %copy.193), channel_id=1, source_target_pairs={{1,0},{2,1},{3,2},{4,3},{5,4},{6,5},{7,6},{8,7},{9,8},{10,9},{11,1... | collective-permute-start | bytes 368648 | tf_op jit(solution)/shard_map/ppermute | solution.py:175
  107.3 31.5 %collective-permute-start.3 = (f32[2,15,1024]{2,0,1:T(2,128)}, f32[2,15,1024]{2,0,1:T(2,128)}, u32[]{:S(2)}, u32[]{:S(2)}) collective-permute-start(f32[2,15,1024]{2,0,1:T(2,128)} %copy.194), channel_id=1, source_target_pairs={{0,1},{1,2},{2,3},{3,4},{4,5},{5,6},{6,7},{7,8},{8,9},{9,10},{10,1... | collective-permute-start | bytes 368648 | tf_op jit(solution)/shard_map/ppermute | solution.py:172
  114.7 8.5 %copy-start.67 = (pred[2,128]{1,0:T(4,128)(4,1)S(1)}, pred[2,128]{1,0:T(4,128)(4,1)}, u32[]{:S(2)}) copy-start(pred[2,128]{1,0:T(4,128)(4,1)} %copy-done.66) | copy-start | bytes 772
  (37 other events, 169.4 us)
Sparse Core Ops, SparseCore 0:
  9.5 15.4 all-gather.2
  26.6 11.7 all-gather.4

commit v2 on v0

--- a/solution.py
+++ b/solution.py
@@ -1,9 +1,253 @@
+import functools
 import math
 
 import jax
 import jax.numpy as jnp
 from jax import lax
+from jax.experimental import pallas as pl
+from jax.experimental.pallas import tpu as pltpu
 from jax.sharding import PartitionSpec as P
+
+MESH = pl.DeviceIdType.MESH
+
+
+FOLD = 2
+
+
+def greet(partners):
+    barrier = pltpu.get_barrier_semaphore()
+    for partner in partners:
+        pl.semaphore_signal(barrier, inc=1, device_id=partner, device_id_type=MESH)
+    pl.semaphore_wait(barrier, len(partners))
+
+
+def reduce_kernel(n_dp, n_seq, count, entries, *refs):
+    far = n_seq // (FOLD * FOLD)
+    ins, outs, rest = refs[:count], refs[count : 2 * count], refs[2 * count :]
+    jobs = len(entries)
+    own, peer, send1, in1, send2, in2, send3, in3, final = (
+        rest[i * jobs : (i + 1) * jobs] for i in range(9)
+    )
+    sems = rest[9 * jobs :]
+    p, q = lax.axis_index("dp"), lax.axis_index("seq")
+    x, y, z = lax.rem(q, FOLD), lax.rem(q // FOLD, FOLD), q // (FOLD * FOLD)
+    x_near = (p, q + 1 - 2 * x)
+    y_near = (p, q + FOLD * (1 - 2 * y))
+    plane = q - z * FOLD * FOLD
+    z_far = [(p, lax.rem(z + 1 + i, far) * FOLD * FOLD + plane) for i in range(far - 1)]
+    dp_far = [(lax.rem(p + 1 + e, n_dp), q) for e in range(n_dp - 1)]
+    greet([*dp_far, x_near, y_near, *z_far])
+    sent = []
+
+    def remote(src, dst, send_sem, recv_sem, target):
+        copy = pltpu.make_async_remote_copy(
+            src_ref=src,
+            dst_ref=dst,
+            send_sem=send_sem,
+            recv_sem=recv_sem,
+            device_id=target,
+            device_id_type=MESH,
+        )
+        copy.start()
+        sent.append(copy)
+        return copy
+
+    def cols(j):
+        return pl.ds(entries[j][1], entries[j][2])
+
+    loads, dp_copies = {}, {}
+    for i in range(far):
+        zz = lax.rem(z + 1 + i, far)
+        for j in range(jobs):
+            a = entries[j][0]
+            for e in range(n_dp - 1):
+                dp_copies[i, j, e] = remote(
+                    ins[a].at[dp_far[e][0], zz, :, :, :, cols(j)],
+                    peer[j].at[e, i],
+                    sems[0].at[j, e, i],
+                    sems[1].at[j, e, i],
+                    dp_far[e],
+                )
+            loads[i, j] = pltpu.make_async_copy(
+                ins[a].at[p, zz, :, :, :, cols(j)], own[j].at[i], sems[2].at[j, i]
+            )
+            loads[i, j].start()
+
+    def base(j, i, row, col):
+        total = own[j][i, row, col].astype(jnp.float32)
+        for e in range(n_dp - 1):
+            total = total + peer[j][e, i, row, col].astype(jnp.float32)
+        return total
+
+    def at(j, first, second):
+        return (second, first) if entries[j][3] else (first, second)
+
+    steps1, steps2, steps3 = {}, {}, {}
+
+    def stage1(j, i):
+        loads[i, j].wait()
+        for e in range(n_dp - 1):
+            dp_copies[i, j, e].wait_recv()
+        mine = x if entries[j][3] else y
+        for other in range(FOLD):
+            send1[j][i, other] = base(j, i, *at(j, 1 - mine, other)).astype(send1[j].dtype)
+        steps1[i, j] = remote(
+            send1[j].at[i],
+            in1[j].at[i],
+            sems[3].at[j, i],
+            sems[4].at[j, i],
+            x_near if entries[j][3] else y_near,
+        )
+
+    def stage2(j, i):
+        steps1[i, j].wait_recv()
+        mine, other = (x, 1 - y) if entries[j][3] else (y, 1 - x)
+        total = base(j, i, *at(j, mine, other)) + in1[j][i, other].astype(jnp.float32)
+        send2[j][i] = total.astype(send2[j].dtype)
+        steps2[i, j] = remote(
+            send2[j].at[i],
+            in2[j].at[i],
+            sems[5].at[j, i],
+            sems[6].at[j, i],
+            y_near if entries[j][3] else x_near,
+        )
+
+    def stage3(j, i):
+        steps2[i, j].wait_recv()
+        mine, other = (x, y) if entries[j][3] else (y, x)
+        total = (
+            base(j, i, *at(j, mine, other))
+            + in1[j][i, other].astype(jnp.float32)
+            + in2[j][i].astype(jnp.float32)
+        )
+        if i < far - 1:
+            send3[j][i] = total.astype(send3[j].dtype)
+            steps3[i, j] = remote(
+                send3[j].at[i], in3[j].at[i], sems[7].at[j, i], sems[8].at[j, i], z_far[i]
+            )
+            return
+        for i in range(far - 1):
+            steps3[i, j].wait_recv()
+            total = total + in3[j][i].astype(jnp.float32)
+        final[j][...] = total.astype(final[j].dtype)
+
+    for step in range(far + 1):
+        for j in range(jobs):
+            if step < far:
+                stage1(j, step)
+        for j in range(jobs):
+            if 1 <= step < far + 1:
+                stage2(j, step - 1)
+        for j in range(jobs):
+            if 2 <= step:
+                stage3(j, step - 2)
+
+    def place(j, zz, yy, xx):
+        return outs[entries[j][0]].at[zz, yy, xx, :, cols(j)]
+
+    keeps, hops_z, hops1, hops2 = [], {}, {}, {}
+
+    def forward(j, i, src, zz):
+        here = place(j, zz, y, x)
+        hops1[i, j] = remote(
+            src, here, sems[11].at[j, i], sems[12].at[j, i], y_near if entries[j][3] else x_near
+        )
+        hops2[i, j, 0] = remote(
+            src,
+            here,
+            sems[13].at[j, 0, i],
+            sems[14].at[j, 0, i],
+            x_near if entries[j][3] else y_near,
+        )
+
+    for j in range(jobs):
+        stage3(j, far - 1)
+        here = place(j, z, y, x)
+        for i in range(far - 1):
+            hops_z[i, j] = remote(final[j], here, sems[9].at[j, i], sems[10].at[j, i], z_far[i])
+        forward(j, far - 1, final[j], z)
+        keep = pltpu.make_async_copy(final[j], here, sems[15].at[j])
+        keep.start()
+        keeps.append(keep)
+
+    def relay(j, i, zz):
+        hops1[i, j].wait_recv()
+        there = place(j, zz, *((1 - y, x) if entries[j][3] else (y, 1 - x)))
+        hops2[i, j, 1] = remote(
+            there,
+            there,
+            sems[13].at[j, 1, i],
+            sems[14].at[j, 1, i],
+            x_near if entries[j][3] else y_near,
+        )
+
+    order = [far - 1, *range(far - 1)]
+    for at_step, i in enumerate(order):
+        if i < far - 1:
+            zz = lax.rem(z + far - 1 - i, far)
+            for j in range(jobs):
+                hops_z[i, j].wait_recv()
+                forward(j, i, place(j, zz, y, x), zz)
+        if at_step:
+            last = order[at_step - 1]
+            for j in range(jobs):
+                relay(j, last, lax.rem(z + 2 * far - 1 - last, far))
+    for j in range(jobs):
+        relay(j, order[-1], lax.rem(z + 2 * far - 1 - order[-1], far))
+    for copy in hops2.values():
+        copy.wait_recv()
+    for keep in keeps:
+        keep.wait()
+    for copy in sent:
+        copy.wait_send()
+
+
+def reduce_all(parts):
+    n_dp, n_seq = lax.axis_size("dp"), lax.axis_size("seq")
+    far = n_seq // (FOLD * FOLD)
+    count = len(parts)
+    parts = [part.reshape(n_dp, far, FOLD, FOLD, *part.shape[2:]) for part in parts]
+    entries = []
+    for a, part in enumerate(parts):
+        wide = part.shape[-1]
+        if wide % 256:
+            entries.append((a, 0, wide, True))
+        else:
+            entries.append((a, 0, wide // 2, True))
+            entries.append((a, wide // 2, wide // 2, False))
+    jobs = len(entries)
+    dma = pltpu.SemaphoreType.DMA
+
+    def slots(*lead):
+        return [
+            pltpu.VMEM((*lead, parts[a].shape[4], size), parts[a].dtype)
+            for a, _, size, _ in entries
+        ]
+
+    results = pl.pallas_call(
+        functools.partial(reduce_kernel, n_dp, n_seq, count, tuple(entries)),
+        out_shape=[jax.ShapeDtypeStruct(part.shape[1:], part.dtype) for part in parts],
+        in_specs=[pl.BlockSpec(memory_space=pl.ANY)] * count,
+        out_specs=[pl.BlockSpec(memory_space=pl.ANY)] * count,
+        scratch_shapes=(
+            slots(far, FOLD, FOLD)
+            + slots(n_dp - 1, far, FOLD, FOLD)
+            + slots(far, FOLD)
+            + slots(far, FOLD)
+            + slots(far)
+            + slots(far)
+            + slots(far)
+            + slots(far)
+            + slots()
+            + [dma((jobs, n_dp - 1, far))] * 2
+            + [dma((jobs, far))] * 11
+            + [dma((jobs, 2, far))] * 2
+            + [dma((jobs,))]
+        ),
+        compiler_params=pltpu.CompilerParams(collective_id=0, has_side_effects=True),
+        name="reduce_all",
+    )(*parts)
+    return [result.reshape(n_seq, *result.shape[3:]) for result in results]
 
 
 def padded(block, sides, width):
@@ -137,22 +381,31 @@
         .astype(jnp.bfloat16)
         .reshape(slabs, frames_dev, width)
     )
-    grad_gain = jnp.stack([grad_gain_pre, grad_gain_mid], axis=1)
-    shares = (
-        lax.psum_scatter(grad_in_w, "dp", scatter_dimension=0, tiled=True),
-        lax.psum_scatter(grad_out_w, "dp", scatter_dimension=0, tiled=True),
-        lax.psum_scatter(grad_taps, "dp", scatter_dimension=0, tiled=True),
-        lax.psum_scatter(grad_gain, "dp", scatter_dimension=0, tiled=True),
-    )
-    totals = lax.psum((shares[0], shares[1], shares[2], shares[3]), "seq")
-    scale = 1.0 / math.sqrt(lax.axis_size("dp") * lax.axis_size("seq") * rows_dev)
+    n_dp, n_seq = lax.axis_size("dp"), lax.axis_size("seq")
+    held = width // n_dp
+    piece = held // n_seq
+    smalls = jnp.concatenate([grad_taps.T, grad_gain_pre[None], grad_gain_mid[None]], axis=0)
+    lines = smalls.shape[0]
+    per_dev = lines * held // n_seq
+    small_rows = -(-per_dev // 1024) * 8
+    smalls = smalls.reshape(lines, n_dp, held).transpose(1, 0, 2).reshape(n_dp, n_seq, per_dev)
+    smalls = jnp.pad(smalls, ((0, 0), (0, 0), (0, small_rows * 128 - per_dev)))
+    sum_in, sum_out, sum_small = reduce_all(
+        (
+            grad_in_w.astype(jnp.bfloat16).reshape(n_dp, n_seq, piece, 2 * width),
+            grad_out_w.astype(jnp.bfloat16).reshape(n_dp, n_seq, piece, width),
+            smalls.reshape(n_dp, n_seq, small_rows, 128),
+        )
+    )
+    scale = 1.0 / math.sqrt(n_dp * n_seq * rows_dev)
+    small = sum_small.reshape(n_seq, -1)[:, :per_dev].reshape(lines, held).T * scale
     return (
         encoded,
         grad_frames,
-        totals[0] * scale,
-        totals[1] * scale,
-        totals[2] * scale,
-        totals[3] * scale,
+        sum_in.reshape(held, 2 * width).astype(jnp.float32) * scale,
+        sum_out.reshape(held, width).astype(jnp.float32) * scale,
+        small[:, :kernel_len],
+        small[:, kernel_len:],
     )
 
 

time: 573 us -> 277 us (0.48)
  waiting for transfers between devices: 401 us -> 39.5 us
  Pallas kernels: 0 us -> 79 us
    psum x2 -> x0, waiting for transfers between devices: 319 us -> none  [per_device(): totals = lax.psum((shares[0], shares[1], shares[2], shares[3]), 'seq')]
    pallas_call x0 -> x1, Pallas kernels: none -> 79 us  [reduce_all(): pl.pallas_call(functools.partial(reduce_kernel, n_dp, n_seq, count, tuple...]
    reduce_scatter x3 -> x0, waiting for transfers between devices: 42.1 us -> none  [the longest x1 19.9 us: per_device(): lax.psum_scatter(grad_in_w, 'dp', scatter_dimension=0, tiled=True)]
  transfers between devices with their start and end apart: 13 -> 7, of which waited for: 7 -> 2; matrix products, arithmetic and copies ran while one was open for 13% -> 21% of each run, Pallas kernels for 0% -> 0%
where the time goes in v2:
time: 277 us; the launch traced here: 276 us
  other arithmetic  82.1 us (30%)
  Pallas kernels  79 us (29%)
  waiting for transfers between devices  39.5 us (14%)
  local copies, waits for them, and re-layouts  20.4 us (7%)
  starting transfers between devices  18.4 us (7%)
  matrix products  17.5 us (6%)
  between operations  15.4 us (6%)
  blocking collectives  3.78 us (1%)
    pallas_call x1, Pallas kernels, reduce_all(): pl.pallas_call(functools.partial(reduce_kernel, n_dp, n_seq, count, tuple...  79 us
    add x1, other arithmetic, per_device(): grad_gated + jnp.where(back_same, grad_pad[:, mirror:mirror + frames_dev]...  28.7 us
    reduce_sum x6, other arithmetic, per_device(): jnp.sum(jnp.where(same, grad_cells * gated_pad[:, tap_index:tap_index + f...  22.2 us
    ppermute x2, waiting for transfers between devices, padded(): lax.ppermute(lax.slice_in_dim(block, block.shape[dim] - width, None, axis...  20.1 us
    all_to_all x1, waiting for transfers between devices, per_device(): lax.all_to_all(outgoing, ('dp', 'seq'), split_axis=0, concat_axis=0, tile...  18 us
    reduce_sum x2, other arithmetic, norm_rows(): average = jnp.mean(values, axis=-1, keepdims=True)  15.4 us
    ppermute x2, starting transfers between devices, padded(): lax.ppermute(lax.slice_in_dim(block, block.shape[dim] - width, None, axis...  6.87 us
    all_to_all x1, starting transfers between devices, per_device(): lax.all_to_all(outgoing, ('dp', 'seq'), split_axis=0, concat_axis=0, tile...  6.19 us
  transfers between devices with their start and end apart: 7, of which 2 were waited for; matrix products, arithmetic and copies ran while one was open for 21% of the time, Pallas kernels for 0%

profile of v2, /device:TPU:19, one launch (start us, length us, event | category | flops | bytes accessed | tf_op | source)
XLA Modules:
  0.0 276.2 jit_solution(10365688810979475059)
XLA Ops:
  7.2 0.7 all-gather.3.cloned.1.call-update
  8.4 2.1 gather_fusion
  10.6 1.2 select_select_fusion
  11.8 6.2 %all-to-all-start = ((bf16[32,16,1024]{2,1,0:T(8,128)(2,1)}), bf16[32,16,1024]{2,1,0:T(8,128)(2,1)S(1)}, u32[]{:S(2)}, u32[]{:S(2)}) async-start(bf16[32,16,1024]{2,1,0:T(8,128)(2,1)} %select_select_fusion), calls=%async_computation | async-start | bytes 2097152 | tf_op jit(solution)/shard_map/all_to_all | solution.py:298
  18.0 0.7 all-gather.5.cloned.1.call-update
  19.1 1.9 all_gather.12
  21.0 1.9 all_gather.14
  22.9 0.7 fusion.294
  23.7 0.8 fusion.295
  24.9 18.0 %all-to-all-done = bf16[32,16,1024]{2,1,0:T(8,128)(2,1)S(1)} async-done(((bf16[32,16,1024]{2,1,0:T(8,128)(2,1)}), bf16[32,16,1024]{2,1,0:T(8,128)(2,1)S(1)}, u32[]{:S(2)}, u32[]{:S(2)}) %all-to-all-start) | async-done | bytes 1048608 | tf_op jit(solution)/shard_map/all_to_all | solution.py:298
  43.0 1.2 gather_fusion.1
  44.8 3.6 %fusion.331 = f32[256,2048]{1,0:T(8,128)S(1)} fusion(bf16[1024,2048]{1,0:T(8,128)(2,1)} %all-gather.3.cloned.1.call-done, f32[1024]{0:T(1024)S(1)} %bitcast.161, f32[256]{0:T(256)S(1)} %fusion.322, f32[256]{0:T(256)S(1)} %broadcast_multiply_fusion.1, bf16[256,1024]{1,0:T(8,128)(2,1)S(1)} %gather_fusion.1, pred[256]{0:T(512)(128)(4,1)S(1)} %compare_and_fusion.1), kind=kOutput, calls=%fused_computation.597 | convolution fusion | flops 1075314688 | bytes 6822144 | tf_op jit(solution)/shard_map/dot_general | solution.py:322
  48.7 1.0 copy-done.1
  50.2 3.0 %collective-permute-start = (bf16[2,15,1024]{1,2,0:T(8,128)(2,1)S(1)}, bf16[2,15,1024]{1,2,0:T(8,128)(2,1)S(1)}, u32[]{:S(2)}, u32[]{:S(2)}) collective-permute-start(bf16[2,15,1024]{1,2,0:T(8,128)(2,1)S(1)} %get-tuple-element.69), channel_id=1, source_target_pairs={{0,1},{1,2},{2,3},{3,4},{4,5},{5,6},{6,7},{7,8},{8,9},{9,10},{10,1... | collective-permute-start | bytes 184328 | tf_op jit(solution)/shard_map/ppermute | solution.py:258
  53.3 2.2 collective-permute-start.1
  55.5 0.7 fusion.296
  56.3 20.1 %collective-permute-done = bf16[2,15,1024]{1,2,0:T(8,128)(2,1)S(1)} collective-permute-done((bf16[2,15,1024]{1,2,0:T(8,128)(2,1)S(1)}, bf16[2,15,1024]{1,2,0:T(8,128)(2,1)S(1)}, u32[]{:S(2)}, u32[]{:S(2)}) %collective-permute-start) | collective-permute-done | bytes 61472 | tf_op jit(solution)/shard_map/ppermute | solution.py:258
  77.2 15.2 %fusion.336 = (f32[2,128]{1,0:T(2,128)S(1)}, f32[2,128,1024]{1,2,0:T(8,128)S(1)}) fusion(f32[1024]{0:T(1024)S(1)} %bitcast.188, bf16[2,15,1024]{1,2,0:T(8,128)(2,1)S(1)} %collective-permute-done.1, bf16[2,128,1024]{1,2,0:T(8,128)(2,1)S(1)} %copy.148, pred[2,128]{1,0:T(4,128)(4,1)} %get-tuple-element.130, f32[1024]{0:T(1024)S(1)} %bitcast.186, ...), kind=kLoop, calls=%fused_computation.600 | loop fusion | flops 55836416 | bytes 1831424 | tf_op jit(solution)/shard_map/jvp()/reduce_sum | solution.py:267
  92.4 1.3 copy.153
  94.0 4.0 %multiply_reduce_fusion = (f32[1024]{0:T(1024)}, f32[256]{0:T(256)S(1)}, f32[256,1024]{1,0:T(8,128)S(1)}) fusion(f32[2,128,1024]{2,1,0:T(8,128)} %copy.153, f32[256]{0:T(256)S(1)} %bitcast_rsqrt_fusion, f32[256]{0:T(256)S(1)} %get-tuple-element.133, f32[1024]{0:T(1024)S(1)} %bitcast.258, bf16[256,1024]{1,0:T(8,128)(2,1)} %bitcast.155, ...), kind=kOutput, calls=%fused_computation.449 | convolution fusion | flops 541326080 | bytes 4729856 | tf_op jit(solution)/shard_map/dot_general | solution.py:345
  98.0 1.4 fusion.334
  99.5 1.3 multiply_reduce_fusion.1
  100.8 1.5 copy.155
  102.4 1.0 fusion.341
  103.5 3.0 %collective-permute-start.2 = (f32[2,15,1024]{2,0,1:T(2,128)S(1)}, f32[2,15,1024]{2,0,1:T(2,128)S(1)}, u32[]{:S(2)}, u32[]{:S(2)}) collective-permute-start(f32[2,15,1024]{2,0,1:T(2,128)S(1)} %copy.193), channel_id=1, source_target_pairs={{1,0},{2,1},{3,2},{4,3},{5,4},{6,5},{7,6},{8,7},{9,8},{10,9},{11,1... | collective-permute-start | bytes 368648 | tf_op jit(solution)/shard_map/ppermute | solution.py:261
  106.5 0.7 copy.194
  107.3 3.8 %collective-permute-start.3 = (f32[2,15,1024]{2,0,1:T(2,128)}, f32[2,15,1024]{2,0,1:T(2,128)}, u32[]{:S(2)}, u32[]{:S(2)}) collective-permute-start(f32[2,15,1024]{2,0,1:T(2,128)} %copy.194), channel_id=1, source_target_pairs={{0,1},{1,2},{2,3},{3,4},{4,5},{5,6},{6,7},{7,8},{8,9},{9,10},{10,1... | collective-permute-start | bytes 368648 | tf_op jit(solution)/shard_map/ppermute | solution.py:258
  111.1 3.5 %bitcast_convert_fusion = bf16[1024,1024]{1,0:T(8,128)(2,1)} fusion(bf16[2,128,1024]{2,1,0:T(8,128)(2,1)} %param.15, f32[2,128,1024]{1,2,0:T(8,128)} %copy-done.4, f32[1024]{0:T(1024)S(1)} %bitcast.260, f32[2,128]{1,0:T(2,128)S(1)} %fusion.323, f32[2,128]{1,0:T(2,128)S(1)} %get-tuple-element.134), kind=kOutput, calls=%fused_computation.58 | convolution fusion | flops 540016640 | bytes 3676160 | tf_op jit(solution)/shard_map/dot_general | solution.py:347
  114.8 4.3 %fusion.128 = (f32[1024]{0:T(1024)S(1)}, f32[1024]{0:T(1024)S(1)}, f32[1024]{0:T(1024)S(1)}, f32[1024]{0:T(1024)S(1)}, f32[1024]{0:T(1024)S(1)}, /*index=5*/f32[1024]{0:T(1024)S(1)}) fusion(f32[2,128,1024]{1,2,0:T(8,128)S(1)} %copy.155, pred[2,128]{1,0:T(4,128)(4,1)} %get-tuple-element.130, bf16[2,15,1024]{1,2,0:T(8,128)(2,1)S(1)} %copy-done.6, ...), kind=kLoop, calls=%fused_computation.312 | loop fusion | flops 11003904 | bytes 1660416 | tf_op jit(solution)/shard_map/reduce_sum | solution.py:356
  119.1 4.1 %fusion.125 = (f32[1024]{0:T(1024)S(1)}, f32[1024]{0:T(1024)S(1)}, f32[1024]{0:T(1024)S(1)}, f32[1024]{0:T(1024)S(1)}, f32[1024]{0:T(1024)S(1)}, /*index=5*/f32[1024]{0:T(1024)S(1)}) fusion(f32[2,128,1024]{1,2,0:T(8,128)S(1)} %copy.155, pred[2,128]{1,0:T(4,128)(4,1)S(1)} %get-tuple-element.103, bf16[2,15,1024]{1,2,0:T(8,128)(2,1)S(1)} %copy-done.6, ...), kind=kLoop, calls=%fused_computation.309 | loop fusion | flops 11003904 | bytes 1660416 | tf_op jit(solution)/shard_map/reduce_sum | solution.py:356
  123.3 4.2 %fusion.77 = (f32[1024]{0:T(1024)S(1)}, f32[1024]{0:T(1024)S(1)}, f32[1024]{0:T(1024)S(1)}, f32[1024]{0:T(1024)S(1)}, f32[1024]{0:T(1024)S(1)}, /*index=5*/f32[1024]{0:T(1024)S(1)}) fusion(f32[2,128,1024]{1,2,0:T(8,128)S(1)} %copy.155, pred[2,128]{1,0:T(4,128)(4,1)} %get-tuple-element.117, bf16[2,128,1024]{1,2,0:T(8,128)(2,1)S(1)} %copy.148, ...), kind=kLoop, calls=%fused_computation.261 | loop fusion | flops 11003904 | bytes 1660416 | tf_op jit(solution)/shard_map/reduce_sum | solution.py:356
  127.5 4.4 %fusion.59 = (f32[1024]{0:T(1024)S(1)}, f32[1024]{0:T(1024)S(1)}, f32[1024]{0:T(1024)S(1)}, f32[1024]{0:T(1024)S(1)}, f32[1024]{0:T(1024)S(1)}, /*index=5*/f32[1024]{0:T(1024)S(1)}) fusion(f32[2,128,1024]{1,2,0:T(8,128)S(1)} %copy.155, pred[2,128]{1,0:T(4,128)(4,1)} %get-tuple-element.124, bf16[2,128,1024]{1,2,0:T(8,128)(2,1)S(1)} %copy.148, ...), kind=kLoop, calls=%fused_computation.243 | loop fusion | flops 11003904 | bytes 1660416 | tf_op jit(solution)/shard_map/reduce_sum | solution.py:356
  131.9 4.0 %fusion.86 = (f32[1024]{0:T(1024)S(1)}, f32[1024]{0:T(1024)S(1)}, f32[1024]{0:T(1024)S(1)}, f32[1024]{0:T(1024)S(1)}, f32[1024]{0:T(1024)S(1)}, /*index=5*/f32[1024]{0:T(1024)S(1)}) fusion(f32[2,128,1024]{1,2,0:T(8,128)S(1)} %copy.155, pred[2,128]{1,0:T(4,128)(4,1)} %get-tuple-element.114, bf16[2,15,1024]{1,2,0:T(8,128)(2,1)S(1)} %copy-done.6, ...), kind=kLoop, calls=%fused_computation.270 | loop fusion | flops 11003904 | bytes 1721856 | tf_op jit(solution)/shard_map/reduce_sum | solution.py:356
  135.9 1.5 fusion.4
  137.8 0.6 concatenate.91
  138.8 2.2 copy.159
  141.1 28.7 %fusion.137 = f32[2,128,1024]{1,2,0:T(8,128)} fusion(f32[2,15,1024]{1,2,0:T(8,128)} %copy.159, f32[2,128,1024]{1,2,0:T(8,128)S(1)} %copy.155, f32[2,15,1024]{1,2,0:T(8,128)S(1)} %copy.156, f32[1024]{0:T(1024)} %bitcast.189, f32[1024]{0:T(1024)} %bitcast.187, f32[1024]{0:T(1024)} %bitcast.185, f32[1024]{0:T(1024)} %bitcast.183, f32[1024]{0:T(1024)S(1)} %bitcast.181, ...), kind=kLoop, calls=%fused_computation.321 | loop fusion | flops 31719424 | bytes 2477568 | tf_op jit(solution)/shard_map/add | solution.py:368
  169.8 2.7 copy.161
  172.5 1.7 fusion.254
  174.3 3.5 %convolution_convert_fusion = bf16[1024,2048]{1,0:T(8,128)(2,1)} fusion(bf16[256,1024]{1,0:T(8,128)(2,1)S(1)} %get-tuple-element.65, bf16[256,1024]{1,0:T(8,128)(2,1)S(1)} %get-tuple-element.64, f32[1024]{0:T(1024)S(1)} %bitcast.162, f32[256]{0:T(256)S(1)} %copy-done.46, f32[256]{0:T(256)S(1)} %copy-done.39, bf16[256,1024]{1,0:T(8,128)(2,1)S(1)} %gather_fusion.1, ...), kind=kOutput, calls=%fused_computation.60 | convolution fusion | flops 1079508992 | bytes 5773568 | tf_op jit(solution)/shard_map/dot_general | solution.py:376
  177.8 1.4 fusion.130
  180.1 0.8 copy.195
  180.9 79.0 %reduce_all.1 = (bf16[4,2,2,32,2048]{4,3,2,1,0:T(8,128)(2,1)}, bf16[4,2,2,32,1024]{4,3,2,1,0:T(8,128)(2,1)}, f32[4,2,2,16,128]{4,3,2,1,0:T(8,128)}) custom-call(bf16[2,4,2,2,32,2048]{5,4,3,2,1,0:T(8,128)(2,1)} %bitcast.148, bf16[2,4,2,2,32,1024]{5,4,3,2,1,0:T(8,128)(2,1)} %bitcast.149, f32[2,4,2,2,16,128]{5,4,3,2,1,0:T(8,128)} %bitcast.152), custom_call_target="tpu_custom_call" | custom-call | tf_op jit(solution)/shard_map/reduce_all/pallas_call | solution.py:227
  259.9 0.9 copy.198
  261.0 0.6 slice.872
  262.2 4.3 %convert_multiply_fusion = f32[4,2,2,32,2048]{4,3,2,1,0:T(8,128)} fusion(bf16[4,2,2,32,2048]{4,3,2,1,0:T(8,128)(2,1)} %get-tuple-element.9), kind=kLoop, calls=%fused_computation.59 | loop fusion | flops 2097152 | bytes 6291456 | tf_op jit(solution)/shard_map/mul | solution.py:405
  266.5 1.6 convert_multiply_fusion.1
  268.1 1.3 add_convert_fusion
  (211 shorter events, 6.1 us)
Async XLA Ops:
  7.2 37.6 %all-gather.3.cloned.1.call-start = ((), (), s32[]{:S(2)}) async-start(), calls=%async_computation.1 | async-start | bytes 6291456 | tf_op jit(solution)/shard_map/all_gather | solution.py:319
  11.8 9.2 %copy-start.35 = (bf16[512,31]{0,1:T(8,128)(2,1)S(1)}, bf16[512,31]{0,1:T(8,128)(2,1)}, u32[]{:S(2)}) copy-start(bf16[512,31]{0,1:T(8,128)(2,1)} %param.13) | copy-start | bytes 95236
  11.8 11.1 %copy-start.11 = (s32[2,2048]{1,0:T(2,128)S(1)}, s32[2,2048]{1,0:T(2,128)}, u32[]{:S(2)}) copy-start(s32[2,2048]{1,0:T(2,128)} %param.10) | copy-start | bytes 49156
  11.8 31.2 %all-to-all-start = ((bf16[32,16,1024]{2,1,0:T(8,128)(2,1)}), bf16[32,16,1024]{2,1,0:T(8,128)(2,1)S(1)}, u32[]{:S(2)}, u32[]{:S(2)}) async-start(bf16[32,16,1024]{2,1,0:T(8,128)(2,1)} %select_select_fusion), calls=%async_computation | async-start | bytes 2097152 | tf_op jit(solution)/shard_map/all_to_all | solution.py:298
  18.0 76.0 %all-gather.5.cloned.1.call-start = ((), (), s32[]{:S(2)}) async-start(), calls=%async_computation.2 | async-start | bytes 3145728 | tf_op jit(solution)/shard_map/all_gather | solution.py:320
  23.7 21.1 %copy-start.40 = (pred[256]{0:T(512)(128)(4,1)}, pred[256]{0:T(512)(128)(4,1)S(1)}, u32[]{:S(2)}) copy-start(pred[256]{0:T(512)(128)(4,1)S(1)} %compare_and_fusion.1) | copy-start | bytes 772
  24.5 51.9 %copy-start.48 = (pred[2,128]{1,0:T(4,128)(4,1)}, pred[2,128]{1,0:T(4,128)(4,1)S(1)}, u32[]{:S(2)}) copy-start(pred[2,128]{1,0:T(4,128)(4,1)S(1)} %get-tuple-element.104) | copy-start | bytes 772
  24.5 51.9 %copy-start.50 = (pred[2,128]{1,0:T(4,128)(4,1)}, pred[2,128]{1,0:T(4,128)(4,1)S(1)}, u32[]{:S(2)}) copy-start(pred[2,128]{1,0:T(4,128)(4,1)S(1)} %get-tuple-element.105) | copy-start | bytes 772
  24.5 51.9 %copy-start.52 = (pred[2,128]{1,0:T(4,128)(4,1)}, pred[2,128]{1,0:T(4,128)(4,1)S(1)}, u32[]{:S(2)}) copy-start(pred[2,128]{1,0:T(4,128)(4,1)S(1)} %get-tuple-element.106) | copy-start | bytes 772
  24.5 51.9 %copy-start.54 = (pred[2,128]{1,0:T(4,128)(4,1)}, pred[2,128]{1,0:T(4,128)(4,1)S(1)}, u32[]{:S(2)}) copy-start(pred[2,128]{1,0:T(4,128)(4,1)S(1)} %get-tuple-element.107) | copy-start | bytes 772
  24.5 51.9 %copy-start.56 = (pred[2,128]{1,0:T(4,128)(4,1)}, pred[2,128]{1,0:T(4,128)(4,1)S(1)}, u32[]{:S(2)}) copy-start(pred[2,128]{1,0:T(4,128)(4,1)S(1)} %get-tuple-element.108) | copy-start | bytes 772
  24.5 51.9 %copy-start.58 = (pred[2,128]{1,0:T(4,128)(4,1)}, pred[2,128]{1,0:T(4,128)(4,1)S(1)}, u32[]{:S(2)}) copy-start(pred[2,128]{1,0:T(4,128)(4,1)S(1)} %get-tuple-element.109) | copy-start | bytes 772
  24.5 51.9 %copy-start.60 = (pred[2,128]{1,0:T(4,128)(4,1)}, pred[2,128]{1,0:T(4,128)(4,1)S(1)}, u32[]{:S(2)}) copy-start(pred[2,128]{1,0:T(4,128)(4,1)S(1)} %get-tuple-element.110) | copy-start | bytes 772
  24.5 51.9 %copy-start.62 = (pred[2,128]{1,0:T(4,128)(4,1)}, pred[2,128]{1,0:T(4,128)(4,1)S(1)}, u32[]{:S(2)}) copy-start(pred[2,128]{1,0:T(4,128)(4,1)S(1)} %get-tuple-element.111) | copy-start | bytes 772
  24.6 51.9 %copy-start.64 = (pred[2,128]{1,0:T(4,128)(4,1)}, pred[2,128]{1,0:T(4,128)(4,1)S(1)}, u32[]{:S(2)}) copy-start(pred[2,128]{1,0:T(4,128)(4,1)S(1)} %get-tuple-element.112) | copy-start | bytes 772
  24.6 94.5 %copy-start.47 = (pred[2,128]{1,0:T(4,128)(4,1)}, pred[2,128]{1,0:T(4,128)(4,1)S(1)}, u32[]{:S(2)}) copy-start(pred[2,128]{1,0:T(4,128)(4,1)S(1)} %get-tuple-element.103) | copy-start | bytes 772
  24.6 51.9 %copy-start.12 = (f32[1024,1]{0,1:T(1,128)}, f32[1024,1]{0,1:T(1,128)S(1)}, u32[]{:S(2)}) copy-start(f32[1024,1]{0,1:T(1,128)S(1)} %get-tuple-element.98) | copy-start | bytes 12292
  24.6 51.9 %copy-start.13 = (f32[1024,1]{0,1:T(1,128)}, f32[1024,1]{0,1:T(1,128)S(1)}, u32[]{:S(2)}) copy-start(f32[1024,1]{0,1:T(1,128)S(1)} %get-tuple-element.99) | copy-start | bytes 12292
  24.7 51.9 %copy-start.14 = (f32[1024,1]{0,1:T(1,128)}, f32[1024,1]{0,1:T(1,128)S(1)}, u32[]{:S(2)}) copy-start(f32[1024,1]{0,1:T(1,128)S(1)} %get-tuple-element.100) | copy-start | bytes 12292
  24.7 51.9 %copy-start.15 = (f32[1024,1]{0,1:T(1,128)}, f32[1024,1]{0,1:T(1,128)S(1)}, u32[]{:S(2)}) copy-start(f32[1024,1]{0,1:T(1,128)S(1)} %get-tuple-element.101) | copy-start | bytes 12292
  24.7 51.8 %copy-start.16 = (f32[1024,1]{0,1:T(1,128)}, f32[1024,1]{0,1:T(1,128)S(1)}, u32[]{:S(2)}) copy-start(f32[1024,1]{0,1:T(1,128)S(1)} %get-tuple-element.71) | copy-start | bytes 12292
  24.8 51.8 %copy-start.17 = (f32[1024,1]{0,1:T(1,128)}, f32[1024,1]{0,1:T(1,128)S(1)}, u32[]{:S(2)}) copy-start(f32[1024,1]{0,1:T(1,128)S(1)} %get-tuple-element.72) | copy-start | bytes 12292
  24.8 51.8 %copy-start.18 = (f32[1024,1]{0,1:T(1,128)}, f32[1024,1]{0,1:T(1,128)S(1)}, u32[]{:S(2)}) copy-start(f32[1024,1]{0,1:T(1,128)S(1)} %get-tuple-element.73) | copy-start | bytes 12292
  24.8 51.8 %copy-start.19 = (f32[1024,1]{0,1:T(1,128)}, f32[1024,1]{0,1:T(1,128)S(1)}, u32[]{:S(2)}) copy-start(f32[1024,1]{0,1:T(1,128)S(1)} %get-tuple-element.74) | copy-start | bytes 12292
  24.8 51.8 %copy-start.20 = (f32[1024,1]{0,1:T(1,128)}, f32[1024,1]{0,1:T(1,128)S(1)}, u32[]{:S(2)}) copy-start(f32[1024,1]{0,1:T(1,128)S(1)} %get-tuple-element.75) | copy-start | bytes 12292
  24.8 51.8 %copy-start.21 = (f32[1024,1]{0,1:T(1,128)}, f32[1024,1]{0,1:T(1,128)S(1)}, u32[]{:S(2)}) copy-start(f32[1024,1]{0,1:T(1,128)S(1)} %get-tuple-element.76) | copy-start | bytes 12292
  24.8 51.8 %copy-start.22 = (f32[1024,1]{0,1:T(1,128)}, f32[1024,1]{0,1:T(1,128)S(1)}, u32[]{:S(2)}) copy-start(f32[1024,1]{0,1:T(1,128)S(1)} %get-tuple-element.77) | copy-start | bytes 12292
  24.8 51.8 %copy-start.23 = (f32[1024,1]{0,1:T(1,128)}, f32[1024,1]{0,1:T(1,128)S(1)}, u32[]{:S(2)}) copy-start(f32[1024,1]{0,1:T(1,128)S(1)} %get-tuple-element.78) | copy-start | bytes 12292
  24.8 51.8 %copy-start.24 = (f32[1024,1]{0,1:T(1,128)}, f32[1024,1]{0,1:T(1,128)S(1)}, u32[]{:S(2)}) copy-start(f32[1024,1]{0,1:T(1,128)S(1)} %get-tuple-element.79) | copy-start | bytes 12292
  24.8 51.8 %copy-start.25 = (f32[1024,1]{0,1:T(1,128)}, f32[1024,1]{0,1:T(1,128)S(1)}, u32[]{:S(2)}) copy-start(f32[1024,1]{0,1:T(1,128)S(1)} %get-tuple-element.80) | copy-start | bytes 12292
  24.8 51.8 %copy-start.26 = (f32[1024,1]{0,1:T(1,128)}, f32[1024,1]{0,1:T(1,128)S(1)}, u32[]{:S(2)}) copy-start(f32[1024,1]{0,1:T(1,128)S(1)} %get-tuple-element.81) | copy-start | bytes 12292
  24.9 51.8 %copy-start.27 = (f32[1024,1]{0,1:T(1,128)}, f32[1024,1]{0,1:T(1,128)S(1)}, u32[]{:S(2)}) copy-start(f32[1024,1]{0,1:T(1,128)S(1)} %get-tuple-element.82) | copy-start | bytes 12292
  24.9 51.8 %copy-start.28 = (f32[1024,1]{0,1:T(1,128)}, f32[1024,1]{0,1:T(1,128)S(1)}, u32[]{:S(2)}) copy-start(f32[1024,1]{0,1:T(1,128)S(1)} %get-tuple-element.83) | copy-start | bytes 12292
  24.9 51.8 %copy-start.29 = (f32[1024,1]{0,1:T(1,128)}, f32[1024,1]{0,1:T(1,128)S(1)}, u32[]{:S(2)}) copy-start(f32[1024,1]{0,1:T(1,128)S(1)} %get-tuple-element.84) | copy-start | bytes 12292
  24.9 51.8 %copy-start.30 = (f32[1024,1]{0,1:T(1,128)}, f32[1024,1]{0,1:T(1,128)S(1)}, u32[]{:S(2)}) copy-start(f32[1024,1]{0,1:T(1,128)S(1)} %get-tuple-element.85) | copy-start | bytes 12292
  24.9 51.8 %copy-start.31 = (f32[1024,1]{0,1:T(1,128)}, f32[1024,1]{0,1:T(1,128)S(1)}, u32[]{:S(2)}) copy-start(f32[1024,1]{0,1:T(1,128)S(1)} %get-tuple-element.86) | copy-start | bytes 12292
  24.9 51.8 %copy-start.32 = (f32[1024,1]{0,1:T(1,128)}, f32[1024,1]{0,1:T(1,128)S(1)}, u32[]{:S(2)}) copy-start(f32[1024,1]{0,1:T(1,128)S(1)} %get-tuple-element.87) | copy-start | bytes 12292
  24.9 51.8 %copy-start.33 = (f32[1024,1]{0,1:T(1,128)}, f32[1024,1]{0,1:T(1,128)S(1)}, u32[]{:S(2)}) copy-start(f32[1024,1]{0,1:T(1,128)S(1)} %get-tuple-element.88) | copy-start | bytes 12292
  24.9 51.8 %copy-start.34 = (f32[1024,1]{0,1:T(1,128)}, f32[1024,1]{0,1:T(1,128)S(1)}, u32[]{:S(2)}) copy-start(f32[1024,1]{0,1:T(1,128)S(1)} %get-tuple-element.89) | copy-start | bytes 12292
  50.2 26.2 %collective-permute-start = (bf16[2,15,1024]{1,2,0:T(8,128)(2,1)S(1)}, bf16[2,15,1024]{1,2,0:T(8,128)(2,1)S(1)}, u32[]{:S(2)}, u32[]{:S(2)}) collective-permute-start(bf16[2,15,1024]{1,2,0:T(8,128)(2,1)S(1)} %get-tuple-element.69), channel_id=1, source_target_pairs={{0,1},{1,2},{2,3},{3,4},{4,5},{5,6},{6,7},{7,8},{8,9},{9,10},{10,1... | collective-permute-start | bytes 184328 | tf_op jit(solution)/shard_map/ppermute | solution.py:258
  53.3 23.1 %collective-permute-start.1 = (bf16[2,15,1024]{1,2,0:T(8,128)(2,1)S(1)}, bf16[2,15,1024]{1,2,0:T(8,128)(2,1)S(1)}, u32[]{:S(2)}, u32[]{:S(2)}) collective-permute-start(bf16[2,15,1024]{1,2,0:T(8,128)(2,1)S(1)} %get-tuple-element.70), channel_id=1, source_target_pairs={{1,0},{2,1},{3,2},{4,3},{5,4},{6,5},{7,6},{8,7},{9,8},{10,9},{11,1... | collective-permute-start | bytes 184328 | tf_op jit(solution)/shard_map/ppermute | solution.py:261
  56.3 37.5 %copy-start.66 = (pred[2,128]{1,0:T(4,128)(4,1)}, pred[2,128]{1,0:T(4,128)(4,1)S(1)}, u32[]{:S(2)}) copy-start(pred[2,128]{1,0:T(4,128)(4,1)S(1)} %get-tuple-element.120) | copy-start | bytes 772
  56.3 37.5 %copy-start.68 = (pred[2,128]{1,0:T(4,128)(4,1)}, pred[2,128]{1,0:T(4,128)(4,1)S(1)}, u32[]{:S(2)}) copy-start(pred[2,128]{1,0:T(4,128)(4,1)S(1)} %get-tuple-element.121) | copy-start | bytes 772
  56.3 37.5 %copy-start.70 = (pred[2,128]{1,0:T(4,128)(4,1)}, pred[2,128]{1,0:T(4,128)(4,1)S(1)}, u32[]{:S(2)}) copy-start(pred[2,128]{1,0:T(4,128)(4,1)S(1)} %get-tuple-element.122) | copy-start | bytes 772
  56.3 37.5 %copy-start.72 = (pred[2,128]{1,0:T(4,128)(4,1)}, pred[2,128]{1,0:T(4,128)(4,1)S(1)}, u32[]{:S(2)}) copy-start(pred[2,128]{1,0:T(4,128)(4,1)S(1)} %get-tuple-element.123) | copy-start | bytes 772
  103.5 35.0 %collective-permute-start.2 = (f32[2,15,1024]{2,0,1:T(2,128)S(1)}, f32[2,15,1024]{2,0,1:T(2,128)S(1)}, u32[]{:S(2)}, u32[]{:S(2)}) collective-permute-start(f32[2,15,1024]{2,0,1:T(2,128)S(1)} %copy.193), channel_id=1, source_target_pairs={{1,0},{2,1},{3,2},{4,3},{5,4},{6,5},{7,6},{8,7},{9,8},{10,9},{11,1... | collective-permute-start | bytes 368648 | tf_op jit(solution)/shard_map/ppermute | solution.py:261
  107.3 31.5 %collective-permute-start.3 = (f32[2,15,1024]{2,0,1:T(2,128)}, f32[2,15,1024]{2,0,1:T(2,128)}, u32[]{:S(2)}, u32[]{:S(2)}) collective-permute-start(f32[2,15,1024]{2,0,1:T(2,128)} %copy.194), channel_id=1, source_target_pairs={{0,1},{1,2},{2,3},{3,4},{4,5},{5,6},{6,7},{7,8},{8,9},{9,10},{10,1... | collective-permute-start | bytes 368648 | tf_op jit(solution)/shard_map/ppermute | solution.py:258
  114.7 8.5 %copy-start.67 = (pred[2,128]{1,0:T(4,128)(4,1)S(1)}, pred[2,128]{1,0:T(4,128)(4,1)}, u32[]{:S(2)}) copy-start(pred[2,128]{1,0:T(4,128)(4,1)} %copy-done.66) | copy-start | bytes 772
  (37 other events, 169.4 us)
Sparse Core Ops, SparseCore 0:
  9.5 15.4 all-gather.2
  26.6 11.7 all-gather.4

commit v3 on v2

--- a/solution.py
+++ b/solution.py
@@ -250,6 +250,96 @@
     return [result.reshape(n_seq, *result.shape[3:]) for result in results]
 
 
+TILE = 16
+LANES = 128
+
+
+def spread(source, target, frames, taps):
+    for shift in range(min(8, taps)):
+        rows = frames + 8 * ((taps - 1 - shift) // 8)
+        for s in range(source.shape[0]):
+            target[shift, s, :rows, :] = source[s, shift : shift + rows, :]
+
+
+def tap_rows(ref, s, row, k, lanes):
+    start = pl.multiple_of(row + 8 * (k // 8), 8)
+    return ref[k % 8, s, pl.ds(start, TILE), lanes]
+
+
+def mix_kernel(id_ref, gated_ref, tap_ref, out_ref, ids, gated):
+    slabs, frames, width = out_ref.shape
+    taps = tap_ref.shape[0]
+    spread(id_ref, ids, frames, taps)
+    spread(gated_ref, gated, frames, taps)
+    every = pl.ds(0, LANES)
+
+    @pl.loop(0, slabs)
+    def _(s):
+        @pl.loop(0, frames // TILE)
+        def _(tile):
+            row = pl.multiple_of(tile * TILE, TILE)
+            center = tap_rows(ids, s, row, taps // 2, every)
+            totals = [jnp.zeros((TILE, LANES), jnp.float32) for _ in range(width // LANES)]
+            for k in range(taps):
+                same = tap_rows(ids, s, row, k, every) == center
+                for c in range(width // LANES):
+                    lanes = pl.ds(c * LANES, LANES)
+                    term = tap_rows(gated, s, row, k, lanes) * tap_ref[k : k + 1, lanes]
+                    totals[c] = totals[c] + jnp.where(same, term, 0.0)
+            for c in range(width // LANES):
+                out_ref[s, pl.ds(row, TILE), pl.ds(c * LANES, LANES)] = totals[c]
+
+
+def unmix_kernel(
+    id_ref, gated_ref, grad_ref, tap_ref, out_ref, tap_out_ref, sums, ids, gated, grad
+):
+    slabs, frames, width = out_ref.shape
+    taps = tap_ref.shape[0]
+    margin = taps // 2
+    spread(id_ref, ids, frames, taps)
+    spread(gated_ref, gated, frames, taps)
+    spread(grad_ref, grad, frames, taps)
+    sums[...] = jnp.zeros_like(sums)
+    every = pl.ds(0, LANES)
+
+    @pl.loop(0, slabs)
+    def _(s):
+        @pl.loop(0, frames // TILE)
+        def _(tile):
+            row = pl.multiple_of(tile * TILE, TILE)
+            center = tap_rows(ids, s, row, margin, every)
+            totals = [jnp.zeros((TILE, LANES), jnp.float32) for _ in range(width // LANES)]
+            for k in range(taps):
+                same = tap_rows(ids, s, row, k, every) == center
+                mirror = taps - 1 - k
+                for c in range(width // LANES):
+                    lanes = pl.ds(c * LANES, LANES)
+                    term = tap_rows(grad, s, row, k, lanes) * tap_ref[mirror : mirror + 1, lanes]
+                    totals[c] = totals[c] + jnp.where(same, term, 0.0)
+                    here = tap_rows(grad, s, row, margin, lanes)
+                    cross = jnp.where(same, here * tap_rows(gated, s, row, k, lanes), 0.0)
+                    folded = cross[:8]
+                    for piece in range(8, TILE, 8):
+                        folded = folded + cross[piece : piece + 8]
+                    sums[k, :, lanes] = sums[k, :, lanes] + folded
+            for c in range(width // LANES):
+                out_ref[s, pl.ds(row, TILE), pl.ds(c * LANES, LANES)] = totals[c]
+
+    for k in range(taps):
+        tap_out_ref[k : k + 1, :] = jnp.sum(sums[k], axis=0, keepdims=True)
+
+
+def local_call(kernel, out_shape, scratch, *args):
+    whole = pl.BlockSpec(memory_space=pltpu.VMEM)
+    return pl.pallas_call(
+        kernel,
+        out_shape=out_shape,
+        in_specs=[whole] * len(args),
+        out_specs=jax.tree.map(lambda _: whole, out_shape),
+        scratch_shapes=scratch,
+    )(*args)
+
+
 def padded(block, sides, width):
     for axis, dim in sides:
         count = lax.axis_size(axis)
@@ -328,16 +418,20 @@
     window = lax.dynamic_slice_in_dim(
         id_pad, lax.axis_index("seq") * frames_dev, frames_dev + 2 * margin, 1
     )
-    center = window[:, margin : margin + frames_dev]
-    mixing = jnp.zeros((slabs, frames_dev, width), jnp.float32)
-    for tap_index in range(kernel_len):
-        same = (window[:, tap_index : tap_index + frames_dev] == center)[..., None]
-        mixing = mixing + jnp.where(
-            same,
-            gated_pad[:, tap_index : tap_index + frames_dev].astype(jnp.float32)
-            * taps[:, tap_index],
-            0.0,
-        )
+    ids = jnp.broadcast_to(window[:, :, None], (*window.shape, LANES))
+    gated_rows = gated_pad.astype(jnp.float32)
+    taps = taps.T
+    reach = frames_dev + 8 * ((kernel_len - 1) // 8)
+    spread_ids = pltpu.VMEM((8, slabs, reach, LANES), jnp.int32)
+    spread_rows = pltpu.VMEM((8, slabs, reach, width), jnp.float32)
+    mixing = local_call(
+        mix_kernel,
+        jax.ShapeDtypeStruct((slabs, frames_dev, width), jnp.float32),
+        [spread_ids, spread_rows],
+        ids,
+        gated_rows,
+        taps,
+    )
     activated_full, pull_mid = jax.vjp(mid_section, mixing.reshape(rows_dev, width), gain_mid)
     activated = activated_full.astype(jnp.bfloat16)
     upstream_rows = upstream.reshape(rows_dev, width)
@@ -348,27 +442,23 @@
     grad_mixing, grad_gain_mid = pull_mid(grad_act)
     grad_cells = grad_mixing.reshape(slabs, frames_dev, width)
     grad_pad = padded(grad_cells, (("seq", 1),), margin)
-    grad_gated = jnp.zeros((slabs, frames_dev, width), jnp.float32)
-    tap_grads = []
-    for tap_index in range(kernel_len):
-        same = (window[:, tap_index : tap_index + frames_dev] == center)[..., None]
-        tap_grads.append(
-            jnp.sum(
-                jnp.where(
-                    same,
-                    grad_cells
-                    * gated_pad[:, tap_index : tap_index + frames_dev].astype(jnp.float32),
-                    0.0,
-                ),
-                axis=(0, 1),
-            )
-        )
-        mirror = 2 * margin - tap_index
-        back_same = (window[:, mirror : mirror + frames_dev] == center)[..., None]
-        grad_gated = grad_gated + jnp.where(
-            back_same, grad_pad[:, mirror : mirror + frames_dev] * taps[:, tap_index], 0.0
-        )
-    grad_taps = jnp.stack(tap_grads, axis=1)
+    grad_gated, grad_taps = local_call(
+        unmix_kernel,
+        (
+            jax.ShapeDtypeStruct((slabs, frames_dev, width), jnp.float32),
+            jax.ShapeDtypeStruct((kernel_len, width), jnp.float32),
+        ),
+        [
+            pltpu.VMEM((kernel_len, 8, width), jnp.float32),
+            spread_ids,
+            spread_rows,
+            spread_rows,
+        ],
+        ids,
+        gated_rows,
+        grad_pad,
+        taps,
+    )
     grad_gated = grad_gated.reshape(rows_dev, width)
     grad_hidden = jnp.concatenate(
         [grad_gated * gate_sig, grad_gated * gate_lin * gate_sig * (1.0 - gate_sig)], axis=1
@@ -384,7 +474,7 @@
     n_dp, n_seq = lax.axis_size("dp"), lax.axis_size("seq")
     held = width // n_dp
     piece = held // n_seq
-    smalls = jnp.concatenate([grad_taps.T, grad_gain_pre[None], grad_gain_mid[None]], axis=0)
+    smalls = jnp.concatenate([grad_taps, grad_gain_pre[None], grad_gain_mid[None]], axis=0)
     lines = smalls.shape[0]
     per_dev = lines * held // n_seq
     small_rows = -(-per_dev // 1024) * 8

time: 277 us -> 207 us (0.75)
  other arithmetic: 82.1 us -> 17.4 us
  Pallas kernels: 79 us -> 103 us
  waiting for transfers between devices: 39.5 us -> 25.9 us
  local copies, waits for them, and re-layouts: 20.4 us -> 7.9 us
    add x1 -> x0, other arithmetic: 28.7 us -> none  [per_device(): grad_gated + jnp.where(back_same, grad_pad[:, mirror:mirror + frames_dev]...]
    pallas_call x0 -> x2, Pallas kernels: none -> 24.2 us  [local_call(): pl.pallas_call(kernel, out_shape=out_shape, in_specs=[whole] * len(args),...]
    reduce_sum x6 -> x0, other arithmetic: 22.2 us -> none  [per_device(): jnp.sum(jnp.where(same, grad_cells * gated_pad[:, tap_index:tap_index + f...]
    ppermute x2, waiting for transfers between devices: 20.1 us -> 0.01 us  [padded(): lax.ppermute(lax.slice_in_dim(block, block.shape[dim] - width, None, axis...]
    reduce_sum x2, other arithmetic: 15.4 us -> 1.7 us  [norm_rows(): average = jnp.mean(values, axis=-1, keepdims=True)]
    ppermute x2, waiting for transfers between devices: 0.01 us -> 5.27 us  [padded(): lax.ppermute(lax.slice_in_dim(block, 0, width, axis=dim), axis, backward)]
    add x2 -> x0, local copies, waits for them, and re-layouts: 4.02 us -> none  [the longest x1 2.68 us: per_device(): grad_gated + jnp.where(back_same, grad_pad[:, mirror:mirror + frames_dev]...]
    unnamed x160 -> x32, local copies, waits for them, and re-layouts: 4.57 us -> 1.79 us
  transfers between devices with their start and end apart: 7 -> 7, of which waited for: 2 -> 3; matrix products, arithmetic and copies ran while one was open for 21% -> 9% of each run, Pallas kernels for 0% -> 5%
where the time goes in v3:
time: 207 us; the launch traced here: 205 us
  Pallas kernels  103 us (50%)
  waiting for transfers between devices  25.9 us (13%)
  other arithmetic  17.4 us (8%)
  starting transfers between devices  17 us (8%)
  matrix products  15.3 us (7%)
  between operations  14.4 us (7%)
  local copies, waits for them, and re-layouts  7.9 us (4%)
  blocking collectives  3.78 us (2%)
    pallas_call x1, Pallas kernels, reduce_all(): pl.pallas_call(functools.partial(reduce_kernel, n_dp, n_seq, count, tuple...  79.1 us
    pallas_call x2, Pallas kernels, local_call(): pl.pallas_call(kernel, out_shape=out_shape, in_specs=[whole] * len(args),...  24.2 us
    all_to_all x1, waiting for transfers between devices, per_device(): lax.all_to_all(outgoing, ('dp', 'seq'), split_axis=0, concat_axis=0, tile...  19.2 us
    all_to_all x1, starting transfers between devices, per_device(): lax.all_to_all(outgoing, ('dp', 'seq'), split_axis=0, concat_axis=0, tile...  6.19 us
    ppermute x2, starting transfers between devices, padded(): lax.ppermute(lax.slice_in_dim(block, 0, width, axis=dim), axis, backward)  5.53 us
    ppermute x2, waiting for transfers between devices, padded(): lax.ppermute(lax.slice_in_dim(block, 0, width, axis=dim), axis, backward)  5.27 us
    ppermute x2, starting transfers between devices, padded(): lax.ppermute(lax.slice_in_dim(block, block.shape[dim] - width, None, axis...  5.17 us
  transfers between devices with their start and end apart: 7, of which 3 were waited for; matrix products, arithmetic and copies ran while one was open for 9% of the time, Pallas kernels for 5%

profile of v3, /device:TPU:19, one launch (start us, length us, event | category | flops | bytes accessed | tf_op | source)
XLA Modules:
  0.0 205.1 jit_solution(12243342302048643423)
XLA Ops:
  7.2 0.7 all-gather.3.cloned.1.call-update
  8.1 0.1 reduce.4
  8.4 2.1 %gather_fusion = bf16[512,1024]{1,0:T(8,128)(2,1)S(1)} fusion(bf16[256,1024]{1,0:T(8,128)(2,1)S(1)} %copy-done, s32[1024]{0:T(1024)S(1)} %pad_clamp_fusion.1), kind=kCustom, calls=%fused_computation | custom fusion | bytes 2099200 | tf_op jit(solution)/shard_map/jit(_take)/gather | solution.py:384
  10.6 1.2 select_select_fusion
  11.8 6.2 %all-to-all-start = ((bf16[32,16,1024]{2,1,0:T(8,128)(2,1)}), bf16[32,16,1024]{2,1,0:T(8,128)(2,1)S(1)}, u32[]{:S(2)}, u32[]{:S(2)}) async-start(bf16[32,16,1024]{2,1,0:T(8,128)(2,1)} %select_select_fusion), calls=%async_computation | async-start | bytes 2097152 | tf_op jit(solution)/shard_map/all_to_all | solution.py:388
  18.0 0.7 all-gather.5.cloned.1.call-update
  18.7 0.2 fusion.40
  19.0 0.1 reduce.2
  19.1 1.9 all_gather.12
  21.0 1.9 all_gather.14
  23.0 0.7 convert_bitcast_fusion.tap_ref
  23.7 19.2 %all-to-all-done = bf16[32,16,1024]{2,1,0:T(8,128)(2,1)S(1)} async-done(((bf16[32,16,1024]{2,1,0:T(8,128)(2,1)}), bf16[32,16,1024]{2,1,0:T(8,128)(2,1)S(1)}, u32[]{:S(2)}, u32[]{:S(2)}) %all-to-all-start) | async-done | bytes 1048608 | tf_op jit(solution)/shard_map/all_to_all | solution.py:388
  43.0 1.2 gather_fusion.1
  44.1 0.3 convert_reduce_fusion
  44.4 0.3 fusion.9
  44.7 3.6 %fusion.35 = f32[256,2048]{1,0:T(8,128)S(1)} fusion(bf16[1024,2048]{1,0:T(8,128)(2,1)} %all-gather.3.cloned.1.call-done, f32[1024]{0:T(1024)S(1)} %bitcast.102, f32[256]{0:T(256)S(1)} %fusion.26, f32[256]{0:T(256)S(1)} %broadcast_multiply_fusion.1, bf16[256,1024]{1,0:T(8,128)(2,1)S(1)} %gather_fusion.1, pred[256]{0:T(512)(128)(4,1)S(1)} %compare_and_fusion.1), kind=kOutput, calls=%fused_computation.97 | convolution fusion | flops 1075314688 | bytes 6822144 | tf_op jit(solution)/shard_map/dot_general | solution.py:412
  48.4 0.3 multiply_convert_fusion.2
  48.7 3.1 %collective-permute-start = (bf16[2,15,1024]{2,1,0:T(8,128)(2,1)S(1)}, bf16[2,15,1024]{2,1,0:T(8,128)(2,1)S(1)}, u32[]{:S(2)}, u32[]{:S(2)}) collective-permute-start(bf16[2,15,1024]{2,1,0:T(8,128)(2,1)S(1)} %get-tuple-element.34), channel_id=1, source_target_pairs={{0,1},{1,2},{2,3},{3,4},{4,5},{5,6},{6,7},{7,8},{8,9},{9,10},{10,1... | collective-permute-start | bytes 184328 | tf_op jit(solution)/shard_map/ppermute | solution.py:348
  51.8 2.2 %collective-permute-start.1 = (bf16[2,15,1024]{2,1,0:T(8,128)(2,1)S(1)}, bf16[2,15,1024]{2,1,0:T(8,128)(2,1)S(1)}, u32[]{:S(2)}, u32[]{:S(2)}) collective-permute-start(bf16[2,15,1024]{2,1,0:T(8,128)(2,1)S(1)} %get-tuple-element.35), channel_id=1, source_target_pairs={{1,0},{2,1},{3,2},{4,3},{5,4},{6,5},{7,6},{8,7},{9,8},{10,9},{11,1... | collective-permute-start | bytes 184328 | tf_op jit(solution)/shard_map/ppermute | solution.py:351
  54.1 3.6 %collective-permute-done.1 = bf16[2,15,1024]{2,1,0:T(8,128)(2,1)S(1)} collective-permute-done((bf16[2,15,1024]{2,1,0:T(8,128)(2,1)S(1)}, bf16[2,15,1024]{2,1,0:T(8,128)(2,1)S(1)}, u32[]{:S(2)}, u32[]{:S(2)}) %collective-permute-start.1) | collective-permute-done | bytes 61472 | tf_op jit(solution)/shard_map/ppermute | solution.py:351
  57.7 1.2 maximum_convert_fusion.gated_ref
  58.9 0.8 broadcast_in_dim.87.id_ref
  59.7 9.5 %shard_map.127 = f32[2,128,1024]{2,1,0:T(8,128)} custom-call(s32[2,158,128]{2,1,0:T(8,128)} %broadcast_in_dim.87.id_ref, f32[2,158,1024]{2,1,0:T(8,128)} %maximum_convert_fusion.gated_ref, f32[31,1024]{1,0:T(8,128)} %convert_bitcast_fusion.tap_ref), custom_call_target="tpu_custom_call" | custom-call | tf_op jit(solution)/shard_map/pallas_call | solution.py:334
  69.2 1.4 reduce_sum.118
  70.6 1.5 multiply_reduce_fusion.2
  72.2 2.8 %multiply_reduce_fusion = (f32[1024]{0:T(1024)S(1)}, f32[256]{0:T(256)S(1)}, f32[256,1024]{1,0:T(8,128)S(1)}) fusion(f32[2,128,1024]{2,1,0:T(8,128)S(1)} %copy-done.1, f32[256]{0:T(256)S(1)} %bitcast_rsqrt_fusion, f32[256]{0:T(256)S(1)} %get-tuple-element.38, f32[1024]{0:T(1024)S(1)} %bitcast.108, bf16[256,1024]{1,0:T(8,128)(2,1)S(1)} %bitcast.96, ...), kind=kOutput, calls=%fused_computation.38 | convolution fusion | flops 541326080 | bytes 4729856 | tf_op jit(solution)/shard_map/dot_general | solution.py:439
  75.0 0.7 fusion.38
  75.7 0.1 broadcast_add_fusion
  75.9 2.1 %collective-permute-start.2 = (f32[2,15,1024]{2,1,0:T(8,128)S(1)}, f32[2,15,1024]{2,1,0:T(8,128)S(1)}, u32[]{:S(2)}, u32[]{:S(2)}) collective-permute-start(f32[2,15,1024]{2,1,0:T(8,128)S(1)} %get-tuple-element.32), channel_id=1, source_target_pairs={{0,1},{1,2},{2,3},{3,4},{4,5},{5,6},{6,7},{7,8},{8,9},{9,10},{10,1... | collective-permute-start | bytes 368648 | tf_op jit(solution)/shard_map/ppermute | solution.py:348
  78.0 3.3 %collective-permute-start.3 = (f32[2,15,1024]{2,1,0:T(8,128)S(1)}, f32[2,15,1024]{2,1,0:T(8,128)S(1)}, u32[]{:S(2)}, u32[]{:S(2)}) collective-permute-start(f32[2,15,1024]{2,1,0:T(8,128)S(1)} %get-tuple-element.33), channel_id=1, source_target_pairs={{1,0},{2,1},{3,2},{4,3},{5,4},{6,5},{7,6},{8,7},{9,8},{10,9},{11,1... | collective-permute-start | bytes 368648 | tf_op jit(solution)/shard_map/ppermute | solution.py:351
  81.3 2.3 %bitcast_convert_fusion = bf16[1024,1024]{1,0:T(8,128)(2,1)} fusion(bf16[2,128,1024]{2,1,0:T(8,128)(2,1)S(1)} %copy-done.6, f32[2,128,1024]{2,1,0:T(8,128)S(1)} %copy-done.1, f32[1024]{0:T(1024)S(1)} %bitcast.110, f32[2,128]{1,0:T(2,128)S(1)} %fusion.27, f32[2,128]{1,0:T(2,128)S(1)} %get-tuple-element.39), kind=kOutput, calls=%fused_computation.2 | convolution fusion | flops 540016640 | bytes 3676160 | tf_op jit(solution)/shard_map/dot_general | solution.py:441
  83.6 1.5 fusion.4
  85.2 1.7 collective-permute-done.3
  86.9 1.2 pad_maximum_fusion.grad_ref
  88.1 14.7 %shard_map.128 = (f32[2,128,1024]{2,1,0:T(8,128)}, f32[31,1024]{1,0:T(8,128)}) custom-call(s32[2,158,128]{2,1,0:T(8,128)} %broadcast_in_dim.87.id_ref, f32[2,158,1024]{2,1,0:T(8,128)} %maximum_convert_fusion.gated_ref, f32[2,158,1024]{2,1,0:T(8,128)} %pad_maximum_fusion.grad_ref, f32[31,1024]{1,0:T(8,128)} %convert_bitcast_fusion.tap_ref), custom_call_target="tpu_custom_call" | custom-call | tf_op jit(solution)/shard_map/pallas_call | solution.py:334
  102.8 1.7 fusion.16
  104.5 3.5 %convolution_convert_fusion = bf16[1024,2048]{1,0:T(8,128)(2,1)} fusion(bf16[256,1024]{1,0:T(8,128)(2,1)S(1)} %get-tuple-element.30, bf16[256,1024]{1,0:T(8,128)(2,1)S(1)} %get-tuple-element.29, f32[1024]{0:T(1024)S(1)} %bitcast.103, f32[256]{0:T(256)S(1)} %fusion.26, f32[256]{0:T(256)S(1)} %broadcast_multiply_fusion.1, ...), kind=kOutput, calls=%fused_computation.4 | convolution fusion | flops 1079508992 | bytes 5773568 | tf_op jit(solution)/shard_map/dot_general | solution.py:466
  108.1 1.5 fusion.10
  109.7 0.6 fusion.8
  110.3 0.1 reshape.328
  110.5 0.8 copy.24
  111.3 79.1 %reduce_all.1 = (bf16[4,2,2,32,2048]{4,3,2,1,0:T(8,128)(2,1)}, bf16[4,2,2,32,1024]{4,3,2,1,0:T(8,128)(2,1)}, f32[4,2,2,16,128]{4,3,2,1,0:T(8,128)}) custom-call(bf16[2,4,2,2,32,2048]{5,4,3,2,1,0:T(8,128)(2,1)} %bitcast.89, bf16[2,4,2,2,32,1024]{5,4,3,2,1,0:T(8,128)(2,1)} %bitcast.92, f32[2,4,2,2,16,128]{5,4,3,2,1,0:T(8,128)} %bitcast.94), custom_call_target="tpu_custom_call" | custom-call | tf_op jit(solution)/shard_map/reduce_all/pallas_call | solution.py:227
  190.4 0.9 copy.27
  191.5 0.6 slice.58
  192.1 0.6 slice.57
  192.7 1.3 add_convert_fusion
  194.0 2.6 %convert_multiply_fusion = f32[4,2,2,32,2048]{4,3,2,1,0:T(8,128)} fusion(bf16[4,2,2,32,2048]{4,3,2,1,0:T(8,128)(2,1)S(1)} %copy-done.4), kind=kLoop, calls=%fused_computation.3 | loop fusion | flops 2097152 | bytes 6291456 | tf_op jit(solution)/shard_map/mul | solution.py:495
  196.6 1.6 convert_multiply_fusion.1
  (70 shorter events, 1.3 us)
Async XLA Ops:
  7.2 1.3 copy-start
  7.2 0.8 copy-start.10
  7.2 37.5 %all-gather.3.cloned.1.call-start = ((), (), s32[]{:S(2)}) async-start(), calls=%async_computation.1 | async-start | bytes 6291456 | tf_op jit(solution)/shard_map/all_gather | solution.py:409
  11.8 7.3 %copy-start.12 = (bf16[512,2]{0,1:T(2,128)(2,1)S(1)}, bf16[512,2]{0,1:T(2,128)(2,1)}, u32[]{:S(2)}) copy-start(bf16[512,2]{0,1:T(2,128)(2,1)} %param.14) | copy-start | bytes 6148
  11.8 9.2 %copy-start.9 = (bf16[512,31]{0,1:T(8,128)(2,1)S(1)}, bf16[512,31]{0,1:T(8,128)(2,1)}, u32[]{:S(2)}) copy-start(bf16[512,31]{0,1:T(8,128)(2,1)} %param.13) | copy-start | bytes 95236
  11.8 31.2 %all-to-all-start = ((bf16[32,16,1024]{2,1,0:T(8,128)(2,1)}), bf16[32,16,1024]{2,1,0:T(8,128)(2,1)S(1)}, u32[]{:S(2)}, u32[]{:S(2)}) async-start(bf16[32,16,1024]{2,1,0:T(8,128)(2,1)} %select_select_fusion), calls=%async_computation | async-start | bytes 2097152 | tf_op jit(solution)/shard_map/all_to_all | solution.py:388
  18.0 54.2 %all-gather.5.cloned.1.call-start = ((), (), s32[]{:S(2)}) async-start(), calls=%async_computation.2 | async-start | bytes 3145728 | tf_op jit(solution)/shard_map/all_gather | solution.py:410
  48.4 10.6 %copy-start.2 = (f32[256,2048]{1,0:T(8,128)}, f32[256,2048]{1,0:T(8,128)S(1)}, u32[]{:S(2)}) copy-start(f32[256,2048]{1,0:T(8,128)S(1)} %fusion.35) | copy-start | bytes 6291460
  48.4 5.6 %copy-start.11 = (s32[2,2048]{1,0:T(2,128)S(1)}, s32[2,2048]{1,0:T(2,128)}, u32[]{:S(2)}) copy-start(s32[2,2048]{1,0:T(2,128)} %param.10) | copy-start | bytes 49156
  48.7 5.4 %collective-permute-start = (bf16[2,15,1024]{2,1,0:T(8,128)(2,1)S(1)}, bf16[2,15,1024]{2,1,0:T(8,128)(2,1)S(1)}, u32[]{:S(2)}, u32[]{:S(2)}) collective-permute-start(bf16[2,15,1024]{2,1,0:T(8,128)(2,1)S(1)} %get-tuple-element.34), channel_id=1, source_target_pairs={{0,1},{1,2},{2,3},{3,4},{4,5},{5,6},{6,7},{7,8},{8,9},{9,10},{10,1... | collective-permute-start | bytes 184328 | tf_op jit(solution)/shard_map/ppermute | solution.py:348
  51.8 5.9 %collective-permute-start.1 = (bf16[2,15,1024]{2,1,0:T(8,128)(2,1)S(1)}, bf16[2,15,1024]{2,1,0:T(8,128)(2,1)S(1)}, u32[]{:S(2)}, u32[]{:S(2)}) collective-permute-start(bf16[2,15,1024]{2,1,0:T(8,128)(2,1)S(1)} %get-tuple-element.35), channel_id=1, source_target_pairs={{1,0},{2,1},{3,2},{4,3},{5,4},{6,5},{7,6},{8,7},{9,8},{10,9},{11,1... | collective-permute-start | bytes 184328 | tf_op jit(solution)/shard_map/ppermute | solution.py:351
  59.7 12.5 %copy-start.6 = (bf16[2,128,1024]{2,1,0:T(8,128)(2,1)S(1)}, bf16[2,128,1024]{2,1,0:T(8,128)(2,1)}, u32[]{:S(2)}) copy-start(bf16[2,128,1024]{2,1,0:T(8,128)(2,1)} %param.15) | copy-start | bytes 1572868
  69.2 3.0 %copy-start.1 = (f32[2,128,1024]{2,1,0:T(8,128)S(1)}, f32[2,128,1024]{2,1,0:T(8,128)}, u32[]{:S(2)}) copy-start(f32[2,128,1024]{2,1,0:T(8,128)} %shard_map.127) | copy-start | bytes 3145732
  75.9 9.3 %collective-permute-start.2 = (f32[2,15,1024]{2,1,0:T(8,128)S(1)}, f32[2,15,1024]{2,1,0:T(8,128)S(1)}, u32[]{:S(2)}, u32[]{:S(2)}) collective-permute-start(f32[2,15,1024]{2,1,0:T(8,128)S(1)} %get-tuple-element.32), channel_id=1, source_target_pairs={{0,1},{1,2},{2,3},{3,4},{4,5},{5,6},{6,7},{7,8},{8,9},{9,10},{10,1... | collective-permute-start | bytes 368648 | tf_op jit(solution)/shard_map/ppermute | solution.py:348
  78.0 5.6 %copy-start.14 = (bf16[1024,1024]{1,0:T(8,128)(2,1)S(1)}, bf16[1024,1024]{1,0:T(8,128)(2,1)}, u32[]{:S(2)}) copy-start(bf16[1024,1024]{1,0:T(8,128)(2,1)} %all-gather.5.cloned.1.call-done) | copy-start | bytes 6291460
  78.0 8.8 %collective-permute-start.3 = (f32[2,15,1024]{2,1,0:T(8,128)S(1)}, f32[2,15,1024]{2,1,0:T(8,128)S(1)}, u32[]{:S(2)}, u32[]{:S(2)}) collective-permute-start(f32[2,15,1024]{2,1,0:T(8,128)S(1)} %get-tuple-element.33), channel_id=1, source_target_pairs={{1,0},{2,1},{3,2},{4,3},{5,4},{6,5},{7,6},{8,7},{9,8},{10,9},{11,1... | collective-permute-start | bytes 368648 | tf_op jit(solution)/shard_map/ppermute | solution.py:351
  88.1 14.7 %copy-start.3 = (f32[256,2048]{1,0:T(8,128)S(1)}, f32[256,2048]{1,0:T(8,128)}, u32[]{:S(2)}) copy-start(f32[256,2048]{1,0:T(8,128)} %copy-done.2) | copy-start | bytes 6291460
  104.5 3.5 %copy-start.13 = (bf16[1024,2048]{1,0:T(8,128)(2,1)S(1)}, bf16[1024,2048]{1,0:T(8,128)(2,1)}, u32[]{:S(2)}) copy-start(bf16[1024,2048]{1,0:T(8,128)(2,1)} %all-gather.3.cloned.1.call-done) | copy-start | bytes 12582916
  108.1 1.5 copy-start.8
  111.3 81.5 %copy-start.7 = (bf16[2,128,1024]{2,1,0:T(8,128)(2,1)S(1)}, bf16[2,128,1024]{2,1,0:T(8,128)(2,1)}, u32[]{:S(2)}) copy-start(bf16[2,128,1024]{2,1,0:T(8,128)(2,1)} %param.15) | copy-start | bytes 1572868
  191.5 2.5 %copy-start.4 = (bf16[4,2,2,32,2048]{4,3,2,1,0:T(8,128)(2,1)S(1)}, bf16[4,2,2,32,2048]{4,3,2,1,0:T(8,128)(2,1)}, u32[]{:S(2)}) copy-start(bf16[4,2,2,32,2048]{4,3,2,1,0:T(8,128)(2,1)} %get-tuple-element.13) | copy-start | bytes 6291460
  194.0 2.6 %copy-start.5 = (bf16[4,2,2,32,1024]{4,3,2,1,0:T(8,128)(2,1)S(1)}, bf16[4,2,2,32,1024]{4,3,2,1,0:T(8,128)(2,1)}, u32[]{:S(2)}) copy-start(bf16[4,2,2,32,1024]{4,3,2,1,0:T(8,128)(2,1)} %get-tuple-element.14) | copy-start | bytes 3145732
Sparse Core Ops, SparseCore 0:
  9.5 15.4 all-gather.2
  26.6 11.7 all-gather.4

commit v4 on v3

--- a/solution.py
+++ b/solution.py
@@ -254,11 +254,41 @@
 LANES = 128
 
 
-def spread(source, target, frames, taps):
+def spread(source, target, frames, taps, skip=0):
     for shift in range(min(8, taps)):
         rows = frames + 8 * ((taps - 1 - shift) // 8)
         for s in range(source.shape[0]):
-            target[shift, s, :rows, :] = source[s, shift : shift + rows, :]
+            target[shift, s, :rows, :] = source[s, skip + shift : skip + shift + rows, :]
+
+
+def exchange_edges(block_ref, edges, send_sem, recv_sem):
+    p, q, n_seq = lax.axis_index("dp"), lax.axis_index("seq"), lax.axis_size("seq")
+    frames, border = block_ref.shape[1], edges.shape[2]
+    after = (p, lax.rem(q + 1, n_seq))
+    before = (p, lax.rem(q + n_seq - 1, n_seq))
+    greet([after, before])
+    copies = []
+    for side, (start, target) in enumerate(((frames - border, after), (0, before))):
+        copy = pltpu.make_async_remote_copy(
+            src_ref=block_ref.at[:, pl.ds(start, border)],
+            dst_ref=edges.at[side],
+            send_sem=send_sem.at[side],
+            recv_sem=recv_sem.at[side],
+            device_id=target,
+            device_id_type=MESH,
+        )
+        copy.start()
+        copies.append(copy)
+    return copies
+
+
+def join_edges(block_ref, edges, full_ref, copies):
+    frames, border = block_ref.shape[1], edges.shape[2]
+    full_ref[:, border : border + frames, :] = block_ref[...].astype(jnp.float32)
+    for copy in copies:
+        copy.wait()
+    full_ref[:, :border, :] = edges[0].astype(jnp.float32)
+    full_ref[:, border + frames :, :] = edges[1].astype(jnp.float32)
 
 
 def tap_rows(ref, s, row, k, lanes):
@@ -266,11 +296,15 @@
     return ref[k % 8, s, pl.ds(start, TILE), lanes]
 
 
-def mix_kernel(id_ref, gated_ref, tap_ref, out_ref, ids, gated):
+def mix_kernel(
+    id_ref, block_ref, tap_ref, out_ref, full_ref, ids, gated, edges, send_sem, recv_sem
+):
     slabs, frames, width = out_ref.shape
     taps = tap_ref.shape[0]
+    copies = exchange_edges(block_ref, edges, send_sem, recv_sem)
     spread(id_ref, ids, frames, taps)
-    spread(gated_ref, gated, frames, taps)
+    join_edges(block_ref, edges, full_ref, copies)
+    spread(full_ref, gated, frames, taps, edges.shape[2] - taps // 2)
     every = pl.ds(0, LANES)
 
     @pl.loop(0, slabs)
@@ -291,14 +325,29 @@
 
 
 def unmix_kernel(
-    id_ref, gated_ref, grad_ref, tap_ref, out_ref, tap_out_ref, sums, ids, gated, grad
+    id_ref,
+    gated_ref,
+    block_ref,
+    tap_ref,
+    out_ref,
+    tap_out_ref,
+    sums,
+    ids,
+    gated,
+    grad,
+    full,
+    edges,
+    send_sem,
+    recv_sem,
 ):
     slabs, frames, width = out_ref.shape
     taps = tap_ref.shape[0]
     margin = taps // 2
+    copies = exchange_edges(block_ref, edges, send_sem, recv_sem)
     spread(id_ref, ids, frames, taps)
-    spread(gated_ref, gated, frames, taps)
-    spread(grad_ref, grad, frames, taps)
+    spread(gated_ref, gated, frames, taps, edges.shape[2] - margin)
+    join_edges(block_ref, edges, full, copies)
+    spread(full, grad, frames, taps, edges.shape[2] - margin)
     sums[...] = jnp.zeros_like(sums)
     every = pl.ds(0, LANES)
 
@@ -329,28 +378,17 @@
         tap_out_ref[k : k + 1, :] = jnp.sum(sums[k], axis=0, keepdims=True)
 
 
-def local_call(kernel, out_shape, scratch, *args):
+def conv_call(kernel, channel, out_shape, scratch, *args):
     whole = pl.BlockSpec(memory_space=pltpu.VMEM)
+    dma = pltpu.SemaphoreType.DMA
     return pl.pallas_call(
         kernel,
         out_shape=out_shape,
         in_specs=[whole] * len(args),
-        out_specs=jax.tree.map(lambda _: whole, out_shape),
-        scratch_shapes=scratch,
+        out_specs=[whole] * len(out_shape),
+        scratch_shapes=[*scratch, dma((2,)), dma((2,))],
+        compiler_params=pltpu.CompilerParams(collective_id=channel, has_side_effects=True),
     )(*args)
-
-
-def padded(block, sides, width):
-    for axis, dim in sides:
-        count = lax.axis_size(axis)
-        forward = [(i, i + 1) for i in range(count - 1)]
-        backward = [(target, source) for source, target in forward]
-        low = lax.ppermute(
-            lax.slice_in_dim(block, block.shape[dim] - width, None, axis=dim), axis, forward
-        )
-        high = lax.ppermute(lax.slice_in_dim(block, 0, width, axis=dim), axis, backward)
-        block = jnp.concatenate([low, block, high], axis=dim)
-    return block
 
 
 def norm_rows(values, gain):
@@ -413,23 +451,25 @@
     gate_lin = hidden[:, :width]
     gate_sig = jax.nn.sigmoid(hidden[:, width:])
     gated = (gate_lin * gate_sig).astype(jnp.bfloat16).reshape(slabs, frames_dev, width)
-    gated_pad = padded(gated, (("seq", 1),), margin)
     id_pad = jnp.pad(segment_ids, ((0, 0), (margin, margin)), constant_values=-1)
     window = lax.dynamic_slice_in_dim(
         id_pad, lax.axis_index("seq") * frames_dev, frames_dev + 2 * margin, 1
     )
     ids = jnp.broadcast_to(window[:, :, None], (*window.shape, LANES))
-    gated_rows = gated_pad.astype(jnp.float32)
     taps = taps.T
     reach = frames_dev + 8 * ((kernel_len - 1) // 8)
     spread_ids = pltpu.VMEM((8, slabs, reach, LANES), jnp.int32)
     spread_rows = pltpu.VMEM((8, slabs, reach, width), jnp.float32)
-    mixing = local_call(
+    border = -(-margin // 16) * 16
+    cells = jax.ShapeDtypeStruct((slabs, frames_dev, width), jnp.float32)
+    longer = (slabs, frames_dev + 2 * border, width)
+    mixing, gated_rows = conv_call(
         mix_kernel,
-        jax.ShapeDtypeStruct((slabs, frames_dev, width), jnp.float32),
-        [spread_ids, spread_rows],
+        1,
+        (cells, jax.ShapeDtypeStruct(longer, jnp.float32)),
+        [spread_ids, spread_rows, pltpu.VMEM((2, slabs, border, width), jnp.bfloat16)],
         ids,
-        gated_rows,
+        gated,
         taps,
     )
     activated_full, pull_mid = jax.vjp(mid_section, mixing.reshape(rows_dev, width), gain_mid)
@@ -441,22 +481,21 @@
     grad_out_w = jnp.dot(activated.T, upstream_rows, preferred_element_type=jnp.float32)
     grad_mixing, grad_gain_mid = pull_mid(grad_act)
     grad_cells = grad_mixing.reshape(slabs, frames_dev, width)
-    grad_pad = padded(grad_cells, (("seq", 1),), margin)
-    grad_gated, grad_taps = local_call(
+    grad_gated, grad_taps = conv_call(
         unmix_kernel,
-        (
-            jax.ShapeDtypeStruct((slabs, frames_dev, width), jnp.float32),
-            jax.ShapeDtypeStruct((kernel_len, width), jnp.float32),
-        ),
+        2,
+        (cells, jax.ShapeDtypeStruct((kernel_len, width), jnp.float32)),
         [
             pltpu.VMEM((kernel_len, 8, width), jnp.float32),
             spread_ids,
             spread_rows,
             spread_rows,
+            pltpu.VMEM(longer, jnp.float32),
+            pltpu.VMEM((2, slabs, border, width), jnp.float32),
         ],
         ids,
         gated_rows,
-        grad_pad,
+        grad_cells,
         taps,
     )
     grad_gated = grad_gated.reshape(rows_dev, width)

time: 207 us -> 208 us (level)
  Pallas kernels: 103 us -> 117 us
  starting transfers between devices: 17 us -> 6.27 us
  waiting for transfers between devices: 25.9 us -> 20.6 us
  local copies, waits for them, and re-layouts: 7.9 us -> 10.1 us
    pallas_call x2, Pallas kernels: 24.2 us -> 35.6 us  [conv_call(): pl.pallas_call(kernel, out_shape=out_shape, in_specs=[whole] * len(args),...]
    ppermute x4 -> x0, starting transfers between devices: 10.7 us -> none  [the longest x2 5.53 us: padded(): lax.ppermute(lax.slice_in_dim(block, 0, width, axis=dim), axis, backward)]
    ppermute x4 -> x0, waiting for transfers between devices: 5.28 us -> none  [the longest x2 5.27 us: padded(): lax.ppermute(lax.slice_in_dim(block, 0, width, axis=dim), axis, backward)]
    unnamed x32, local copies, waits for them, and re-layouts: 1.79 us -> 4 us
  transfers between devices with their start and end apart: 7 -> 3, of which waited for: 3 -> 1; matrix products, arithmetic and copies ran while one was open for 9% -> 7% of each run, Pallas kernels for 5% -> 7%
where the time goes in v4:
time: 208 us; the launch traced here: 206 us
  Pallas kernels  117 us (56%)
  waiting for transfers between devices  20.6 us (10%)
  other arithmetic  18.1 us (9%)
  matrix products  16.3 us (8%)
  between operations  14.4 us (7%)
  local copies, waits for them, and re-layouts  10.1 us (5%)
  starting transfers between devices  6.27 us (3%)
  blocking collectives  3.78 us (2%)
    pallas_call x1, Pallas kernels, reduce_all(): pl.pallas_call(functools.partial(reduce_kernel, n_dp, n_seq, count, tuple...  81.2 us
    pallas_call x2, Pallas kernels, conv_call(): pl.pallas_call(kernel, out_shape=out_shape, in_specs=[whole] * len(args),...  35.6 us
    all_to_all x1, waiting for transfers between devices, per_device(): lax.all_to_all(outgoing, ('dp', 'seq'), split_axis=0, concat_axis=0, tile...  19.2 us
    all_to_all x1, starting transfers between devices, per_device(): lax.all_to_all(outgoing, ('dp', 'seq'), split_axis=0, concat_axis=0, tile...  6.19 us
  transfers between devices with their start and end apart: 3, of which 1 were waited for; matrix products, arithmetic and copies ran while one was open for 7% of the time, Pallas kernels for 7%

profile of v4, /device:TPU:19, one launch (start us, length us, event | category | flops | bytes accessed | tf_op | source)
XLA Modules:
  0.0 206.2 jit_solution(17901125409020393842)
XLA Ops:
  7.2 0.7 all-gather.3.cloned.1.call-update
  8.0 0.1 copy.20
  8.1 0.1 reduce.4
  8.3 0.1 min.12
  8.4 2.1 gather_fusion
  10.6 1.2 select_select_fusion
  11.8 6.2 %all-to-all-start = ((bf16[32,16,1024]{2,1,0:T(8,128)(2,1)}), bf16[32,16,1024]{2,1,0:T(8,128)(2,1)S(1)}, u32[]{:S(2)}, u32[]{:S(2)}) async-start(bf16[32,16,1024]{2,1,0:T(8,128)(2,1)} %select_select_fusion), calls=%async_computation | async-start | bytes 2097152 | tf_op jit(solution)/shard_map/all_to_all | solution.py:426
  18.0 0.7 all-gather.5.cloned.1.call-update
  18.7 0.2 fusion.40
  19.0 0.1 reduce.2
  19.1 1.9 all_gather.12
  21.0 1.9 all_gather.14
  22.9 0.1 pad_dynamic-slice_fusion
  23.0 0.1 convert_reduce_fusion.1
  23.1 0.7 convert_bitcast_fusion.tap_ref
  23.8 19.2 %all-to-all-done = bf16[32,16,1024]{2,1,0:T(8,128)(2,1)S(1)} async-done(((bf16[32,16,1024]{2,1,0:T(8,128)(2,1)}), bf16[32,16,1024]{2,1,0:T(8,128)(2,1)S(1)}, u32[]{:S(2)}, u32[]{:S(2)}) %all-to-all-start) | async-done | bytes 1048608 | tf_op jit(solution)/shard_map/all_to_all | solution.py:426
  43.0 1.2 gather_fusion.1
  44.1 0.3 convert_reduce_fusion
  44.4 0.3 fusion.9
  44.7 3.6 %fusion.35 = f32[256,2048]{1,0:T(8,128)S(1)} fusion(bf16[1024,2048]{1,0:T(8,128)(2,1)} %all-gather.3.cloned.1.call-done, f32[1024]{0:T(1024)S(1)} %bitcast.100, f32[256]{0:T(256)S(1)} %fusion.26, f32[256]{0:T(256)S(1)} %broadcast_multiply_fusion.1, bf16[256,1024]{1,0:T(8,128)(2,1)S(1)} %gather_fusion.1, pred[256]{0:T(512)(128)(4,1)S(1)} %compare_and_fusion.1), kind=kOutput, calls=%fused_computation.95 | convolution fusion | flops 1075314688 | bytes 6822144 | tf_op jit(solution)/shard_map/dot_general | solution.py:450
  48.4 1.3 copy-done.2
  49.7 1.1 multiply_convert_fusion.2
  50.8 0.8 broadcast_in_dim.87.id_ref
  51.5 14.9 %shard_map.127 = (f32[2,128,1024]{2,1,0:T(8,128)}, f32[2,160,1024]{2,1,0:T(8,128)}) custom-call(s32[2,158,128]{2,1,0:T(8,128)} %broadcast_in_dim.87.id_ref, bf16[2,128,1024]{2,1,0:T(8,128)(2,1)} %bitcast.90, f32[31,1024]{1,0:T(8,128)} %convert_bitcast_fusion.tap_ref), custom_call_target="tpu_custom_call" | custom-call | tf_op jit(solution)/shard_map/pallas_call | solution.py:384
  66.4 1.4 reduce_sum.118
  67.9 1.5 multiply_reduce_fusion.2
  69.4 2.9 %multiply_reduce_fusion = (f32[1024]{0:T(1024)S(1)}, f32[256]{0:T(256)S(1)}, f32[256,1024]{1,0:T(8,128)S(1)}) fusion(f32[2,128,1024]{2,1,0:T(8,128)S(1)} %copy-done.1, f32[256]{0:T(256)S(1)} %bitcast_rsqrt_fusion, f32[256]{0:T(256)S(1)} %get-tuple-element.38, f32[1024]{0:T(1024)S(1)} %bitcast.106, bf16[256,1024]{1,0:T(8,128)(2,1)S(1)} %bitcast.94, ...), kind=kOutput, calls=%fused_computation.37 | convolution fusion | flops 541326080 | bytes 4729856 | tf_op jit(solution)/shard_map/dot_general | solution.py:479
  72.3 1.4 fusion.38
  73.7 1.1 broadcast_add_fusion
  74.8 20.8 %shard_map.128 = (f32[2,128,1024]{2,1,0:T(8,128)}, f32[31,1024]{1,0:T(8,128)}) custom-call(s32[2,158,128]{2,1,0:T(8,128)} %broadcast_in_dim.87.id_ref, f32[2,160,1024]{2,1,0:T(8,128)} %get-tuple-element.14.gated_ref, f32[2,128,1024]{2,1,0:T(8,128)} %bitcast.88, f32[31,1024]{1,0:T(8,128)} %convert_bitcast_fusion.tap_ref), custom_call_target="tpu_custom_call" | custom-call | tf_op jit(solution)/shard_map/pallas_call | solution.py:384
  95.6 2.4 %fusion.16 = (bf16[256,1024]{1,0:T(8,128)(2,1)S(1)}, bf16[256,1024]{1,0:T(8,128)(2,1)S(1)}) fusion(f32[2,128,1024]{2,1,0:T(8,128)} %get-tuple-element.15, f32[256,2048]{1,0:T(8,128)} %copy-done.2), kind=kLoop, calls=%fused_computation.32 | loop fusion | flops 2621440 | bytes 4194304 | tf_op jit(solution)/shard_map/convert.3
  98.0 3.5 %convolution_convert_fusion = bf16[1024,2048]{1,0:T(8,128)(2,1)} fusion(bf16[256,1024]{1,0:T(8,128)(2,1)S(1)} %get-tuple-element.34, bf16[256,1024]{1,0:T(8,128)(2,1)S(1)} %get-tuple-element.33, f32[1024]{0:T(1024)S(1)} %bitcast.101, f32[256]{0:T(256)S(1)} %fusion.26, f32[256]{0:T(256)S(1)} %broadcast_multiply_fusion.1, ...), kind=kOutput, calls=%fused_computation.4 | convolution fusion | flops 1079508992 | bytes 5773568 | tf_op jit(solution)/shard_map/dot_general | solution.py:505
  101.5 1.5 fusion.10
  103.0 0.1 concatenate.15
  103.1 0.6 fusion.8
  103.7 0.1 reshape.328
  103.9 0.8 copy.24
  104.7 3.3 %bitcast_convert_fusion = bf16[1024,1024]{1,0:T(8,128)(2,1)} fusion(bf16[2,128,1024]{2,1,0:T(8,128)(2,1)} %param.15, f32[2,128,1024]{2,1,0:T(8,128)S(1)} %copy-done.1, f32[1024]{0:T(1024)S(1)} %bitcast.108, f32[2,128]{1,0:T(2,128)S(1)} %fusion.27, f32[2,128]{1,0:T(2,128)S(1)} %get-tuple-element.39), kind=kOutput, calls=%fused_computation.2 | convolution fusion | flops 540016640 | bytes 3676160 | tf_op jit(solution)/shard_map/dot_general | solution.py:481
  108.0 81.2 %reduce_all.1 = (bf16[4,2,2,32,2048]{4,3,2,1,0:T(8,128)(2,1)}, bf16[4,2,2,32,1024]{4,3,2,1,0:T(8,128)(2,1)}, f32[4,2,2,16,128]{4,3,2,1,0:T(8,128)}) custom-call(bf16[2,4,2,2,32,2048]{5,4,3,2,1,0:T(8,128)(2,1)} %bitcast.87, bf16[2,4,2,2,32,1024]{5,4,3,2,1,0:T(8,128)(2,1)} %bitcast.89, f32[2,4,2,2,16,128]{5,4,3,2,1,0:T(8,128)} %bitcast.92), custom_call_target="tpu_custom_call" | custom-call | tf_op jit(solution)/shard_map/reduce_all/pallas_call | solution.py:227
  189.2 0.9 copy.27
  190.1 0.1 mul.256
  190.2 0.6 slice.38
  190.8 0.6 slice.37
  191.5 1.3 add_convert_fusion
  192.7 2.6 %convert_multiply_fusion = f32[4,2,2,32,2048]{4,3,2,1,0:T(8,128)} fusion(bf16[4,2,2,32,2048]{4,3,2,1,0:T(8,128)(2,1)S(1)} %copy-done.3), kind=kLoop, calls=%fused_computation.3 | loop fusion | flops 2097152 | bytes 6291456 | tf_op jit(solution)/shard_map/mul | solution.py:534
  195.3 1.6 convert_multiply_fusion.1
  196.9 0.9 copy-done.14
  197.9 1.5 fusion.4
  (58 shorter events, 0.7 us)
Async XLA Ops:
  7.2 1.3 copy-start
  7.2 0.8 copy-start.10
  7.2 37.5 %all-gather.3.cloned.1.call-start = ((), (), s32[]{:S(2)}) async-start(), calls=%async_computation.1 | async-start | bytes 6291456 | tf_op jit(solution)/shard_map/all_gather | solution.py:447
  11.8 7.3 %copy-start.12 = (bf16[512,2]{0,1:T(2,128)(2,1)S(1)}, bf16[512,2]{0,1:T(2,128)(2,1)}, u32[]{:S(2)}) copy-start(bf16[512,2]{0,1:T(2,128)(2,1)} %param.14) | copy-start | bytes 6148
  11.8 9.2 %copy-start.9 = (bf16[512,31]{0,1:T(8,128)(2,1)S(1)}, bf16[512,31]{0,1:T(8,128)(2,1)}, u32[]{:S(2)}) copy-start(bf16[512,31]{0,1:T(8,128)(2,1)} %param.13) | copy-start | bytes 95236
  11.8 11.1 %copy-start.11 = (s32[2,2048]{1,0:T(2,128)S(1)}, s32[2,2048]{1,0:T(2,128)}, u32[]{:S(2)}) copy-start(s32[2,2048]{1,0:T(2,128)} %param.10) | copy-start | bytes 49156
  11.8 31.2 %all-to-all-start = ((bf16[32,16,1024]{2,1,0:T(8,128)(2,1)}), bf16[32,16,1024]{2,1,0:T(8,128)(2,1)S(1)}, u32[]{:S(2)}, u32[]{:S(2)}) async-start(bf16[32,16,1024]{2,1,0:T(8,128)(2,1)} %select_select_fusion), calls=%async_computation | async-start | bytes 2097152 | tf_op jit(solution)/shard_map/all_to_all | solution.py:426
  18.0 51.4 %all-gather.5.cloned.1.call-start = ((), (), s32[]{:S(2)}) async-start(), calls=%async_computation.2 | async-start | bytes 3145728 | tf_op jit(solution)/shard_map/all_gather | solution.py:448
  48.4 1.3 copy-start.2
  50.8 18.6 %copy-start.6 = (bf16[2,128,1024]{2,1,0:T(8,128)(2,1)S(1)}, bf16[2,128,1024]{2,1,0:T(8,128)(2,1)}, u32[]{:S(2)}) copy-start(bf16[2,128,1024]{2,1,0:T(8,128)(2,1)} %param.15) | copy-start | bytes 1572868
  66.4 3.0 %copy-start.1 = (f32[2,128,1024]{2,1,0:T(8,128)S(1)}, f32[2,128,1024]{2,1,0:T(8,128)}, u32[]{:S(2)}) copy-start(f32[2,128,1024]{2,1,0:T(8,128)} %get-tuple-element.13) | copy-start | bytes 3145732
  98.0 3.5 %copy-start.13 = (bf16[1024,2048]{1,0:T(8,128)(2,1)S(1)}, bf16[1024,2048]{1,0:T(8,128)(2,1)}, u32[]{:S(2)}) copy-start(bf16[1024,2048]{1,0:T(8,128)(2,1)} %all-gather.3.cloned.1.call-done) | copy-start | bytes 12582916
  101.5 1.5 copy-start.8
  108.0 83.5 %copy-start.7 = (bf16[2,128,1024]{2,1,0:T(8,128)(2,1)S(1)}, bf16[2,128,1024]{2,1,0:T(8,128)(2,1)}, u32[]{:S(2)}) copy-start(bf16[2,128,1024]{2,1,0:T(8,128)(2,1)} %param.15) | copy-start | bytes 1572868
  190.2 2.5 %copy-start.3 = (bf16[4,2,2,32,2048]{4,3,2,1,0:T(8,128)(2,1)S(1)}, bf16[4,2,2,32,2048]{4,3,2,1,0:T(8,128)(2,1)}, u32[]{:S(2)}) copy-start(bf16[4,2,2,32,2048]{4,3,2,1,0:T(8,128)(2,1)} %get-tuple-element.17) | copy-start | bytes 6291460
  192.7 2.6 %copy-start.4 = (bf16[4,2,2,32,1024]{4,3,2,1,0:T(8,128)(2,1)S(1)}, bf16[4,2,2,32,1024]{4,3,2,1,0:T(8,128)(2,1)}, u32[]{:S(2)}) copy-start(bf16[4,2,2,32,1024]{4,3,2,1,0:T(8,128)(2,1)} %get-tuple-element.18) | copy-start | bytes 3145732
  195.3 1.6 copy-start.5
  195.3 2.5 %copy-start.14 = (bf16[1024,1024]{1,0:T(8,128)(2,1)S(1)}, bf16[1024,1024]{1,0:T(8,128)(2,1)}, u32[]{:S(2)}) copy-start(bf16[1024,1024]{1,0:T(8,128)(2,1)} %all-gather.5.cloned.1.call-done) | copy-start | bytes 6291460
Sparse Core Ops, SparseCore 0:
  9.5 15.4 all-gather.2
  26.6 11.7 all-gather.4
